TPU v7x, 32 devices: a whole 2x2x4 slice. The times are simulated.
32 devices in a mesh: seg: 4 (over y, x), coil: 8 (over z, core).
Axes of the slice: x: 2, y: 2, z: 4, core: 2. Of those that a mesh axis runs over, the one named last changes fastest.
Arguments:
- image_estimate: bfloat16 [1, 384, 768], replicated, may hold values from -6 to 6
- coil_maps: bfloat16 [8, 384, 768], P('coil'), may hold values from -3 to 3
- field_map: float32 [384, 384], replicated, may hold values from -3 to 3
- interp_rows: bfloat16 [1, 256, 384], replicated, may hold values from -0.3125 to 0.3125
- interp_cols: bfloat16 [1, 128, 384], replicated, may hold values from -0.3125 to 0.3125
- measured: bfloat16 [8, 1, 256, 256], P('coil'), may hold values from -6 to 6
- sample_time: int32 [1, 256], replicated, may hold values from 0 to 12
- sample_count: int32 [1], replicated, may hold values from 128 to 256
Outputs:
- gradient: float32 [1, 384, 768], P(None, 'coil', 'seg')
- residual: float32 [8, 1, 256, 256], P('coil', None, 'seg')
Inputs may be any that keep to these rules, and one draw needn't show every extreme that they name: sample_time counts the sample clock, 4 steps to a segment. Rows below sample_count[p] of partition p are acquired.
All inputs are finite; a program needn't handle non-finite values.
Results may differ from a plain program's by a relative error of at most 0.017.
Values sent between devices are 32-bit elements; how exact they have to be, the bound alone decides.
No kernel may reach another device: no remote copies, remote signals or barrier semaphores. Data moves between devices by JAX's collectives and lax.ppermute only.
A program may use at most 64 MiB of HBM per device.

v0:
```python
import math

import jax
import jax.numpy as jnp
from jax import lax
from jax.sharding import PartitionSpec as P

SUBSTEPS = 4


def dft_tables(length):
    indices = jnp.arange(length, dtype=jnp.int32)
    wrapped = indices[:, None] * indices[None, :] % length
    angles = wrapped.astype(jnp.float32) * (2.0 * math.pi / length)
    factor = 1.0 / math.sqrt(length)
    return (jnp.cos(angles) * factor, jnp.sin(angles) * factor)


def shards(
    image_estimate,
    coil_maps,
    field_map,
    interp_rows,
    interp_cols,
    measured,
    sample_time,
    sample_count,
):
    segment = lax.axis_index("seg")
    seg_total = lax.axis_size("seg")
    coil_total = lax.axis_size("coil")
    pixels = field_map.shape[0]
    row_total = interp_rows.shape[1]
    col_total = interp_cols.shape[1]
    own_rows = row_total // seg_total
    start_row = segment * own_rows
    cosine, sine = dft_tables(pixels)
    stacked_table = jnp.concatenate([cosine, sine], axis=0).astype(jnp.bfloat16)
    forward_right = jnp.concatenate(
        [jnp.concatenate([cosine, -sine], 1), jnp.concatenate([sine, cosine], 1)], 0
    ).astype(jnp.bfloat16)
    inverse_right = jnp.concatenate(
        [jnp.concatenate([cosine, sine], 1), jnp.concatenate([-sine, cosine], 1)], 0
    ).astype(jnp.bfloat16)
    offset = segment.astype(jnp.float32) - 0.5 * (seg_total - 1)
    angles = field_map * offset
    phase_re = jnp.cos(angles)
    phase_im = jnp.sin(angles)
    maps = coil_maps[0].astype(jnp.float32)
    sens_re = maps[:, :pixels]
    sens_im = maps[:, pixels:]
    comb_re = sens_re * phase_re - sens_im * phase_im
    comb_im = sens_re * phase_im + sens_im * phase_re
    factor = coil_total ** (-0.5)
    row_ids = jnp.arange(row_total, dtype=jnp.int32)
    current = image_estimate[0].astype(jnp.float32)
    cur_re = current[:, :pixels]
    cur_im = current[:, pixels:]
    weighted = jnp.concatenate(
        [cur_re * comb_re - cur_im * comb_im, cur_re * comb_im + cur_im * comb_re], 1
    ).astype(jnp.bfloat16)
    products = jnp.dot(stacked_table, weighted, preferred_element_type=jnp.float32)
    cos_part = products[:pixels]
    sin_part = products[pixels:]
    rows_ft = jnp.concatenate(
        [cos_part[:, :pixels] + sin_part[:, pixels:], cos_part[:, pixels:] - sin_part[:, :pixels]],
        1,
    ).astype(jnp.bfloat16)
    kspace = jnp.dot(rows_ft, forward_right, preferred_element_type=jnp.float32).astype(
        jnp.bfloat16
    )
    picked = jnp.dot(interp_rows[0], kspace, preferred_element_type=jnp.float32).astype(
        jnp.bfloat16
    )
    sampled = jnp.einsum(
        "mrn,kn->mrk",
        picked.reshape(row_total, 2, pixels),
        interp_cols[0],
        preferred_element_type=jnp.float32,
    ).reshape(row_total, 2 * col_total)
    sample_steps = sample_time[0].astype(jnp.float32)
    weights = jnp.maximum(
        0.0, 1.0 - jnp.abs(sample_steps - (segment * SUBSTEPS).astype(jnp.float32)) / SUBSTEPS
    )
    partial_sum = weights[:, None] * sampled
    sampled_mask = (row_ids < sample_count[0]).astype(jnp.float32)[:, None]
    data_rows = measured[0, 0].astype(jnp.float32)
    owned_sum = lax.psum_scatter(partial_sum, "seg", scatter_dimension=0, tiled=True)
    mask_own = lax.dynamic_slice_in_dim(sampled_mask, start_row, own_rows, 0)
    data_own = lax.dynamic_slice_in_dim(data_rows, start_row, own_rows, 0)
    misfit_own = mask_own * (owned_sum - data_own)
    misfit = lax.all_gather(misfit_own, "seg", axis=0, tiled=True)
    back_weighted = (weights[:, None] * misfit).astype(jnp.bfloat16)
    spread = lax.dot_general(
        interp_rows[0], back_weighted, (((0,), (0,)), ((), ())), preferred_element_type=jnp.float32
    ).astype(jnp.bfloat16)
    gridded = (
        jnp.einsum(
            "nrk,kj->nrj",
            spread.reshape(pixels, 2, col_total),
            interp_cols[0],
            preferred_element_type=jnp.float32,
        )
        .reshape(pixels, 2 * pixels)
        .astype(jnp.bfloat16)
    )
    back_products = jnp.dot(stacked_table, gridded, preferred_element_type=jnp.float32)
    cos_back = back_products[:pixels]
    sin_back = back_products[pixels:]
    back_rows = jnp.concatenate(
        [cos_back[:, :pixels] - sin_back[:, pixels:], cos_back[:, pixels:] + sin_back[:, :pixels]],
        1,
    ).astype(jnp.bfloat16)
    back_image = jnp.dot(back_rows, inverse_right, preferred_element_type=jnp.float32)
    image_re = back_image[:, :pixels]
    image_im = back_image[:, pixels:]
    image_term = factor * jnp.concatenate(
        [comb_re * image_re + comb_im * image_im, comb_re * image_im - comb_im * image_re], 1
    )
    across = lax.psum_scatter(image_term, "coil", scatter_dimension=0, tiled=True)
    reduced = lax.psum_scatter(across, "seg", scatter_dimension=1, tiled=True)
    gradients = [reduced]
    residuals = [misfit_own]
    gradient = jnp.stack(gradients, axis=0)
    residual = jnp.stack(residuals, axis=0)[None]
    return (gradient, residual)


def solution(mesh):
    in_specs = (P(), P("coil", None, None), P(), P(), P(), P("coil", None, None, None), P(), P())
    out_specs = (P(None, "coil", "seg"), P("coil", None, "seg", None))
    return jax.shard_map(shards, mesh=mesh, in_specs=in_specs, out_specs=out_specs, check_vma=False)
```

profile of v0, /device:TPU:0, one launch (start us, length us, event | category | flops | bytes accessed | tf_op | source)
XLA Modules:
  0.0 128.1 jit_solution(544643491294426139)
XLA Ops:
  7.2 0.0 copy-start
  7.2 0.0 copy-start.2
  7.2 0.0 reduce-scatter.6.cloned.1.call-start
  7.2 2.3 %negate_convert_fusion = bf16[384,384]{1,0:T(8,128)(2,1)S(1)} fusion(), kind=kLoop, calls=%fused_computation.43 | loop fusion | flops 1769472 | bytes 294912 | tf_op jit(solution)/shard_map/convert.15
  9.6 2.6 %multiply_convert_fusion = (bf16[384,384]{1,0:T(8,128)(2,1)S(1)}, bf16[384,384]{1,0:T(8,128)(2,1)S(1)}) fusion(), kind=kLoop, calls=%fused_computation.48 | loop fusion | flops 1916928 | bytes 589824 | tf_op jit(solution)/shard_map/convert.20
  12.2 0.0 copy-done.2
  12.2 0.0 copy-start.1
  12.2 1.3 %bitcast_convert_fusion = (f32[384,768]{1,0:T(8,128)S(1)}, f32[384,768]{1,0:T(8,128)S(1)}) fusion(bf16[1,384,768]{2,1,0:T(8,128)(2,1)S(1)} %copy-done.2, bf16[1,384,768]{2,1,0:T(8,128)(2,1)} %param.9), kind=kLoop, calls=%fused_computation.39 | loop fusion | flops 589824 | bytes 3538944 | tf_op jit(solution)/shard_map/convert_element_type | solution.py:56
  13.5 0.0 copy-done.1
  13.5 2.4 %subtract_convert_fusion = (bf16[384,384]{1,0:T(8,128)(2,1)S(1)}, f32[384,384]{1,0:T(8,128)S(1)}, f32[384,384]{1,0:T(8,128)S(1)}) fusion(f32[384,768]{1,0:T(8,128)S(1)} %get-tuple-element.11, f32[384,768]{1,0:T(8,128)S(1)} %get-tuple-element.12, f32[384,384]{1,0:T(8,128)S(1)} %copy-done.1, f32[]{:T(128)S(6)} %sub.42), kind=kLoop, calls=%fused_computation.45 | loop fusion | flops 1622016 | bytes 4423684 | tf_op jit(solution)/shard_map/convert.18
  15.8 0.2 add_convert_fusion
  16.0 0.8 fusion.20
  16.9 0.1 fusion.19
  17.0 0.0 copy-done
  17.0 0.0 copy-start.3
  17.0 1.3 fusion.1
  18.3 0.0 copy-start.5
  18.3 0.0 copy-done.3
  18.3 0.2 fusion.42
  18.5 0.1 copy.15
  18.7 0.3 copy-done.5
  19.0 0.8 broadcast_multiply_fusion
  19.8 0.0 reduce-scatter.6.cloned.1.call-update
  19.8 0.0 reduce-scatter.8.cloned.1.call-start
  20.5 0.1 dynamic-slice.4
  20.6 26.4 %reduce-scatter.6.cloned.1.call-done = f32[64,256]{1,0:T(8,128)} async-done(((f32[256,256]{1,0:T(8,128)}), f32[64,256]{1,0:T(8,128)}) %reduce-scatter.6.cloned.1.call-update) | async-done | bytes 65552 | tf_op jit(solution)/shard_map/reduce_scatter | solution.py:88
  47.0 0.9 fusion.44
  47.9 0.0 copy-start.4
  47.9 9.3 %all_gather.3 = f32[256,256]{1,0:T(8,128)S(1)} all-gather(f32[64,256]{1,0:T(8,128)S(1)} %fusion.44), channel_id=1, replica_groups=mesh['seg'=4,'coil'=8] {'seg'}, dimensions={0}, use_global_device_ids=true | all-gather | bytes 327680 | tf_op jit(solution)/shard_map/all_gather | solution.py:92
  57.2 0.3 convolution_convert_fusion.2
  57.5 0.4 convolution_convert_fusion
  57.9 0.8 fusion.37
  58.7 0.0 copy-done.4
  58.7 0.1 fusion.17
  58.8 0.7 fusion.6
  59.5 0.2 multiply_add_fusion
  59.7 1.1 maximum_multiply_fusion
  60.8 0.0 reduce-scatter.8.cloned.1.call-update
  60.9 0.0 reduce-scatter.10.cloned.1.call-start
  60.9 33.1 %reduce-scatter.8.cloned.1.call-done = f32[48,768]{1,0:T(8,128)} async-done(((f32[384,768]{1,0:T(8,128)}), f32[48,768]{1,0:T(8,128)}) %reduce-scatter.8.cloned.1.call-update) | async-done | bytes 147472 | tf_op jit(solution)/shard_map/reduce_scatter | solution.py:120
  94.0 1.8 %copy.22 = f32[48,768]{0,1:T(8,128)} copy(f32[48,768]{1,0:T(8,128)} %reduce-scatter.8.cloned.1.call-done) | data formatting | bytes 294912
  95.8 0.0 reduce-scatter.10.cloned.1.call-update
  95.8 24.1 %reduce-scatter.10.cloned.1.call-done = f32[192,48]{1,0:T(8,128)} async-done(((f32[768,48]{1,0:T(8,128)}), f32[192,48]{1,0:T(8,128)}) %reduce-scatter.10.cloned.1.call-update) | async-done | bytes 36880
  119.9 1.6 %copy.23 = f32[48,192]{1,0:T(8,128)} copy(f32[48,192]{0,1:T(8,128)} %bitcast.47) | data formatting | bytes 73728
  (2 shorter events, 0.0 us)
Async XLA Ops:
  7.2 9.8 %copy-start = (bf16[1,256,384]{2,1,0:T(8,128)(2,1)S(1)}, bf16[1,256,384]{2,1,0:T(8,128)(2,1)}, u32[]{:S(2)}) copy-start(bf16[1,256,384]{2,1,0:T(8,128)(2,1)} %param.11) | copy-start | bytes 589828
  7.2 5.0 %copy-start.2 = (bf16[1,384,768]{2,1,0:T(8,128)(2,1)S(1)}, bf16[1,384,768]{2,1,0:T(8,128)(2,1)}, u32[]{:S(2)}) copy-start(bf16[1,384,768]{2,1,0:T(8,128)(2,1)} %param.8) | copy-start | bytes 1769476
  7.2 39.8 %reduce-scatter.6.cloned.1.call-start = ((), (), s32[]{:S(2)}) async-start(), calls=%async_computation.3 | async-start | bytes 327680 | tf_op jit(solution)/shard_map/reduce_scatter | solution.py:88
  12.2 1.3 %copy-start.1 = (f32[384,384]{1,0:T(8,128)S(1)}, f32[384,384]{1,0:T(8,128)}, u32[]{:S(2)}) copy-start(f32[384,384]{1,0:T(8,128)} %param.10) | copy-start | bytes 1769476
  17.0 1.3 %copy-start.3 = (bf16[1,128,384]{2,1,0:T(8,128)(2,1)S(1)}, bf16[1,128,384]{2,1,0:T(8,128)(2,1)}, u32[]{:S(2)}) copy-start(bf16[1,128,384]{2,1,0:T(8,128)(2,1)} %param.12) | copy-start | bytes 294916
  18.3 0.7 copy-start.5
  19.8 74.2 %reduce-scatter.8.cloned.1.call-start = ((), (), s32[]{:S(2)}) async-start(), calls=%async_computation.4 | async-start | bytes 1327104 | tf_op jit(solution)/shard_map/reduce_scatter | solution.py:120
  47.9 10.8 %copy-start.4 = (f32[64,256]{1,0:T(8,128)}, f32[64,256]{1,0:T(8,128)S(1)}, u32[]{:S(2)}) copy-start(f32[64,256]{1,0:T(8,128)S(1)} %fusion.44) | copy-start | bytes 196612
  60.9 59.1 %reduce-scatter.10.cloned.1.call-start = ((), (), s32[]{:S(2)}) async-start(), calls=%async_computation.5 | async-start | bytes 491520
Sparse Core Ops, SparseCore 0:
  19.9 27.0 reduce-scatter.5
  61.0 32.9 reduce-scatter.7
  96.8 23.1 reduce-scatter.9
where the time goes:
time: 128 us
  waiting for transfers between devices  83.6 us (65%)
  between operations  14.6 us (11%)
  other arithmetic  12 us (9%)
  blocking collectives  9.28 us (7%)
  matrix products  4.5 us (4%)
  local copies, waits for them, and re-layouts  3.94 us (3%)
    reduce_scatter x1, waiting for transfers between devices, shards(): lax.psum_scatter(image_term, 'coil', scatter_dimension=0, tiled=True)  33.1 us
    reduce_scatter x1, waiting for transfers between devices, shards(): lax.psum_scatter(partial_sum, 'seg', scatter_dimension=0, tiled=True)  26.4 us
    unnamed x4, waiting for transfers between devices  24.2 us
    all_gather x1, blocking collectives, shards(): misfit = lax.all_gather(misfit_own, 'seg', axis=0, tiled=True)  9.28 us
    another operation x6, other arithmetic  7.65 us
    unnamed x14, local copies, waits for them, and re-layouts  3.73 us
  transfers between devices with their start and end apart: 3, of which 3 were waited for; matrix products, arithmetic and copies ran while one was open for 0% of the time, Pallas kernels for 0%

commit v1 on v0

v1 whole, which is shorter than its diff:
```python
import math

import jax
import jax.numpy as jnp
import numpy as np
from jax import lax
from jax.sharding import PartitionSpec as P

SUBSTEPS = 4


def dft_tables(length):
    wrapped = np.outer(np.arange(length), np.arange(length)) % length
    angles = wrapped * (2.0 * math.pi / length)
    factor = 1.0 / math.sqrt(length)
    return np.cos(angles) * factor, -np.sin(angles) * factor


def dot(a, b):
    return jnp.dot(a, b, preferred_element_type=jnp.float32)


def exchange_sum(blocks, axis):
    total = lax.axis_size(axis)
    me = lax.axis_index(axis)
    lane = me % 2
    group = me // 2
    groups = total // 2
    split = blocks.reshape(groups, 2, *blocks.shape[1:])
    away = lax.dynamic_index_in_dim(split, 1 - lane, 1, False)
    kept = lax.dynamic_index_in_dim(split, lane, 1, False)
    paired = kept + lax.ppermute(away, axis, [(i, i ^ 1) for i in range(total)])
    result = lax.dynamic_index_in_dim(paired, group, 0, False)
    for step in range(1, groups):
        piece = lax.dynamic_index_in_dim(paired, (group + step) % groups, 0, False)
        result = result + lax.ppermute(
            piece, axis, [(i, (i + 2 * step) % total) for i in range(total)]
        )
    return result


def shards(
    image_estimate,
    coil_maps,
    field_map,
    interp_rows,
    interp_cols,
    measured,
    sample_time,
    sample_count,
):
    segment = lax.axis_index("seg")
    seg_total = lax.axis_size("seg")
    coil_total = lax.axis_size("coil")
    pixels = field_map.shape[0]
    row_total = interp_rows.shape[1]
    own_rows = row_total // seg_total
    width = 2 * pixels // seg_total
    column = (segment * width) % pixels
    imaginary = segment * width >= pixels
    fourier_re, fourier_im = dft_tables(pixels)
    fourier = jnp.asarray(np.concatenate([fourier_re, fourier_im], 1), jnp.bfloat16)
    row_op = dot(interp_rows[0], fourier).astype(jnp.bfloat16)
    col_op = dot(interp_cols[0], fourier).astype(jnp.bfloat16)
    row_re, row_im = row_op[:, :pixels], row_op[:, pixels:]
    col_re, col_im = col_op[:, :pixels], col_op[:, pixels:]
    maps = coil_maps[0].astype(jnp.float32)
    sens_re, sens_im = maps[:, :pixels], maps[:, pixels:]
    current = image_estimate[0].astype(jnp.float32)
    cur_re, cur_im = current[:, :pixels], current[:, pixels:]
    base_re = cur_re * sens_re - cur_im * sens_im
    base_im = cur_re * sens_im + cur_im * sens_re
    steps = sample_time[0].astype(jnp.float32)
    col_right = jnp.concatenate(
        [jnp.concatenate([col_re, -col_im], 1), jnp.concatenate([col_im, col_re], 1)], 0
    )
    samples = 0.0
    phases = []
    weights = []
    for s in range(seg_total):
        angles = field_map * (s - 0.5 * (seg_total - 1))
        phase_re, phase_im = jnp.cos(angles), jnp.sin(angles)
        phases.append((phase_re, phase_im))
        weight = jnp.maximum(0.0, 1.0 - jnp.abs(steps - s * SUBSTEPS) / SUBSTEPS)[:, None]
        weights.append(weight)
        weighted = jnp.concatenate(
            [base_re * phase_re - base_im * phase_im, base_re * phase_im + base_im * phase_re], 1
        ).astype(jnp.bfloat16)
        v = lax.dot_general(
            weighted, col_right, (((1,), (1,)), ((), ())), preferred_element_type=jnp.float32
        ).astype(jnp.bfloat16)
        half = v.shape[1] // 2
        turned = jnp.concatenate([-v[:, half:], v[:, :half]], 1)
        samples = samples + weight * dot(
            jnp.concatenate([row_re, row_im], 1), jnp.concatenate([v, turned], 0)
        )
    mask = (jnp.arange(row_total) < sample_count[0]).astype(jnp.float32)[:, None]
    misfit = mask * (samples - measured[0, 0].astype(jnp.float32))
    own = lax.dynamic_slice_in_dim(misfit, segment * own_rows, own_rows, 0)
    part_re = lax.dynamic_slice_in_dim(col_re, column, width, 1)
    part_im = lax.dynamic_slice_in_dim(col_im, column, width, 1)
    col_left = jnp.concatenate(
        [jnp.concatenate([part_re, -part_im], 1), jnp.concatenate([part_im, part_re], 1)], 0
    )
    turned = dot(misfit.astype(jnp.bfloat16), col_left)
    turn_re, turn_im = turned[:, :width], turned[:, width:]
    row_stack = jnp.concatenate([row_re, row_im], 0)
    sum_re = 0.0
    sum_im = 0.0
    for s in range(seg_total):
        top = jnp.concatenate([turn_re, turn_im], 1) * weights[s]
        low = jnp.concatenate([turn_im, -turn_re], 1) * weights[s]
        image = lax.dot_general(
            row_stack,
            jnp.concatenate([top, low], 0).astype(jnp.bfloat16),
            (((0,), (0,)), ((), ())),
            preferred_element_type=jnp.float32,
        )
        image_re, image_im = image[:, :width], image[:, width:]
        phase_re = lax.dynamic_slice_in_dim(phases[s][0], column, width, 1)
        phase_im = lax.dynamic_slice_in_dim(phases[s][1], column, width, 1)
        sum_re = sum_re + phase_re * image_re + phase_im * image_im
        sum_im = sum_im + phase_re * image_im - phase_im * image_re
    map_re = lax.dynamic_slice_in_dim(sens_re, column, width, 1)
    map_im = lax.dynamic_slice_in_dim(sens_im, column, width, 1)
    first = jnp.where(imaginary, -map_im, map_re)
    second = jnp.where(imaginary, map_re, map_im)
    term = coil_total ** (-0.5) * (first * sum_re + second * sum_im)
    gradient = exchange_sum(term.reshape(coil_total, pixels // coil_total, width), "coil")
    return gradient[None], own[None, None]


def solution(mesh):
    in_specs = (P(), P("coil", None, None), P(), P(), P(), P("coil", None, None, None), P(), P())
    out_specs = (P(None, "coil", "seg"), P("coil", None, "seg", None))
    return jax.shard_map(shards, mesh=mesh, in_specs=in_specs, out_specs=out_specs, check_vma=False)
```

time: 128 us -> 45.5 us (0.36)
  waiting for transfers between devices: 83.6 us -> 2.5 us
  between operations: 14.6 us -> 1.76 us
  other arithmetic: 12 us -> 21.3 us
  blocking collectives: 9.28 us -> 0 us
  starting transfers between devices: 0.12 us -> 7.48 us
  local copies, waits for them, and re-layouts: 3.94 us -> 6.94 us
    reduce_scatter x2 -> x0, waiting for transfers between devices: 59.5 us -> none  [the longest x1 33.1 us: shards(): lax.psum_scatter(image_term, 'coil', scatter_dimension=0, tiled=True)]
    unnamed x4 -> x0, waiting for transfers between devices: 24.2 us -> none
    another operation x6 -> x3, other arithmetic: 7.65 us -> 19.6 us
    all_gather x1 -> x0, blocking collectives: 9.28 us -> none  [shards(): misfit = lax.all_gather(misfit_own, 'seg', axis=0, tiled=True)]
    ppermute x0 -> x4, starting transfers between devices: none -> 7.48 us  [the longest x3 6.92 us: exchange_sum(): lax.ppermute(piece, axis, [(i, (i + 2 * step) % total) for i in range(tot...]
    ppermute x0 -> x4, waiting for transfers between devices: none -> 2.5 us  [the longest x3 1.43 us: exchange_sum(): lax.ppermute(piece, axis, [(i, (i + 2 * step) % total) for i in range(tot...]
    mul x3 -> x1, other arithmetic: 2.86 us -> 0.61 us  [shards(): term = coil_total ** (-0.5) * (first * sum_re + second * sum_im)]
    unnamed x14 -> x37, local copies, waits for them, and re-layouts: 3.73 us -> 5.22 us
  transfers between devices with their start and end apart: 3 -> 4, of which waited for: 3 -> 3; matrix products, arithmetic and copies ran while one was open for 0% -> 3% of each run, Pallas kernels for 0% -> 0%
where the time goes in v1:
time: 45.5 us; the launch traced here: 45.3 us
  other arithmetic  21.3 us (47%)
  starting transfers between devices  7.48 us (16%)
  local copies, waits for them, and re-layouts  6.94 us (15%)
  matrix products  5.23 us (11%)
  waiting for transfers between devices  2.5 us (5%)
  between operations  1.76 us (4%)
    another operation x3, other arithmetic  19.6 us
    ppermute x3, starting transfers between devices, exchange_sum(): lax.ppermute(piece, axis, [(i, (i + 2 * step) % total) for i in range(tot...  6.92 us
    unnamed x37, local copies, waits for them, and re-layouts  5.22 us
    dot_general x7, matrix products, dot(): return jnp.dot(a, b, preferred_element_type=jnp.float32)  2.05 us
    dot_general x4, matrix products, shards(): lax.dot_general(row_stack, jnp.concatenate([top, low], 0).astype(jnp.bflo...  1.69 us
    dot_general x4, matrix products, shards(): lax.dot_general(weighted, col_right, (((1,), (1,)), ((), ())), preferred_...  1.48 us
    broadcast_in_dim x1, local copies, waits for them, and re-layouts, shards(): return (gradient[None], own[None, None])  1.47 us
    ppermute x3, waiting for transfers between devices, exchange_sum(): lax.ppermute(piece, axis, [(i, (i + 2 * step) % total) for i in range(tot...  1.43 us
  transfers between devices with their start and end apart: 4, of which 3 were waited for; matrix products, arithmetic and copies ran while one was open for 3% of the time, Pallas kernels for 0%

profile of v1, /device:TPU:0, one launch (start us, length us, event | category | flops | bytes accessed | tf_op | source)
XLA Modules:
  0.0 45.3 jit_solution(1007046846032358085)
XLA Ops:
  0.6 0.0 copy-start
  0.7 1.5 %copy.17 = bf16[1,384,768]{1,2,0:T(8,128)(2,1)S(1)} copy(bf16[1,384,768]{2,1,0:T(8,128)(2,1)} %param.10) | data formatting | bytes 1179648 | tf_op args[1]
  2.2 0.0 copy-start.1
  2.2 0.0 copy-start.14
  2.2 0.3 copy.19
  2.5 0.2 copy.18
  2.8 0.5 %copy-done.1 = bf16[384,768]{1,0:T(8,128)(2,1)S(1)} copy-done((bf16[384,768]{1,0:T(8,128)(2,1)S(1)}, bf16[384,768]{1,0:T(8,128)(2,1)}, u32[]{:S(2)}) %copy-start.1) | copy-done | bytes 589848
  3.2 0.0 copy-done.14
  3.3 0.4 fusion.5
  3.7 0.2 bitcast_convert_fusion
  3.8 10.3 %subtract_convert_fusion = (bf16[384,384]{0,1:T(8,128)(2,1)S(1)}, f32[384,384]{0,1:T(8,128)S(1)}, f32[384,384]{0,1:T(8,128)S(1)}, f32[384,384]{0,1:T(8,128)S(1)}...) fusion(f32[384,384]{0,1:T(8,128)S(1)} %copy.18, ...), kind=kLoop, calls=%fused_computation.31 | loop fusion | flops 2064384 | bytes 10321920 | tf_op jit(solution)/shard_map/convert.11
  14.1 8.9 %add_convert_fusion = (bf16[384,384]{0,1:T(8,128)(2,1)S(1)}, bf16[384,384]{0,1:T(8,128)(2,1)S(1)}, bf16[384,384]{0,1:T(8,128)(2,1)S(1)}, bf16[384,384]{0,1:T(8,1...) fusion(f32[384,384]{0,1:T(8,128)S(1)} %get-tuple-element.4, ...), kind=kLoop, calls=%fused_computation.30 | loop fusion | flops 4718592 | bytes 3833856 | tf_op jit(solution)/shard_map/convert.12
  23.1 0.4 convolution_convert_fusion.4
  23.5 0.4 convolution_convert_fusion
  23.9 0.3 copy-done.15
  24.1 0.4 convolution_convert_fusion.5
  24.6 0.4 convolution_convert_fusion.3
  25.0 0.4 convolution_convert_fusion.2
  26.1 0.3 convolution_multiply_fusion.2
  26.4 0.3 fusion
  26.7 0.3 fusion.1
  26.9 0.6 %copy-done.16 = bf16[1,1,256,256]{3,2,1,0:T(8,128)(2,1)S(1)} copy-done((bf16[1,1,256,256]{3,2,1,0:T(8,128)(2,1)S(1)}, bf16[1,1,256,256]{3,2,1,0:T(8,128)(2,1)}, u32[]{:S(2)}) %copy-start.16) | copy-done | bytes 131096
  27.6 0.3 fusion.4
  27.9 0.7 %copy-done.13 = f32[256,256]{1,0:T(8,128)} copy-done((f32[256,256]{1,0:T(8,128)}, f32[256,256]{1,0:T(8,128)S(1)}, u32[]{:S(2)}) %copy-start.13) | copy-done | bytes 262168
  28.5 0.2 fusion.54
  28.8 0.1 fusion.83
  29.0 0.4 multiply_convert_fusion.7
  29.3 0.4 fusion.38
  29.8 0.4 fusion.42
  30.3 0.4 fusion.46
  30.7 0.4 fusion.50
  31.2 0.1 copy-done.9
  31.2 0.3 copy-done.4
  31.5 0.2 copy-done.5
  31.7 0.2 copy-done.6
  31.9 0.2 copy-done.2
  32.1 0.2 copy-done.3
  32.3 0.6 %add_multiply_fusion = f32[384,192]{0,1:T(8,128)S(1)} fusion(f32[384,384]{0,1:T(8,128)S(1)} %fusion.50, f32[384,384]{0,1:T(8,128)S(1)} %copy-done.10, s32[]{:T(128)S(6)} %select_n.78, f32[384,384]{0,1:T(8,128)S(1)} %copy-done.9, f32[384,384]{0,1:T(8,128)S(1)} %copy-done.8, f32[384,384]{0,1:T(8,128)S(1)} %fusion.46, f32[384,384]{0,1:T(8,128)S(1)} %copy-done.7, ...), kind=kLoop, calls=%fused_computation.95 | loop fusion | flops 2727936 | bytes 5603333 | tf_op jit(solution)/shard_map/mul | solution.py:128
  32.9 0.2 copy.23
  33.1 0.6 %collective-permute-start = (f32[4,48,192]{2,1,0:T(8,128)S(1)}, f32[4,48,192]{2,1,0:T(8,128)S(1)}, u32[]{:S(2)}, u32[]{:S(2)}) collective-permute-start(f32[4,48,192]{2,1,0:T(8,128)S(1)} %dynamic-slice_bitcast_fusion), channel_id=1, source_target_pairs={{0,1},{1,0},{2,3},{3,2},{4,5},{5,4},{6,7},{7,6},{8,9},{9,8},{10,11... | collective-permute-start | bytes 442376 | tf_op jit(solution)/shard_map/ppermute | solution.py:32
  33.7 1.1 %collective-permute-done = f32[4,48,192]{2,1,0:T(8,128)S(1)} collective-permute-done((f32[4,48,192]{2,1,0:T(8,128)S(1)}, f32[4,48,192]{2,1,0:T(8,128)S(1)}, u32[]{:S(2)}, u32[]{:S(2)}) %collective-permute-start) | collective-permute-done | bytes 147488 | tf_op jit(solution)/shard_map/ppermute | solution.py:32
  34.8 3.0 %collective-permute-start.1 = (f32[48,192]{1,0:T(8,128)S(1)}, f32[48,192]{1,0:T(8,128)S(1)}, u32[]{:S(2)}, u32[]{:S(2)}) collective-permute-start(f32[48,192]{1,0:T(8,128)S(1)} %get-tuple-element.36), channel_id=1, source_target_pairs={{0,2},{1,3},{2,4},{3,5},{4,6},{5,7},{6,0},{7,1},{8,10},{9,11},{10,... | collective-permute-start | bytes 110600 | tf_op jit(solution)/shard_map/ppermute | solution.py:36
  37.8 2.6 %collective-permute-start.2 = (f32[48,192]{1,0:T(8,128)S(1)}, f32[48,192]{1,0:T(8,128)S(1)}, u32[]{:S(2)}, u32[]{:S(2)}) collective-permute-start(f32[48,192]{1,0:T(8,128)S(1)} %get-tuple-element.38), channel_id=1, source_target_pairs={{0,4},{1,5},{2,6},{3,7},{4,0},{5,1},{6,2},{7,3},{8,12},{9,13},{10,... | collective-permute-start | bytes 110600 | tf_op jit(solution)/shard_map/ppermute | solution.py:36
  40.4 1.3 %collective-permute-start.3 = (f32[48,192]{1,0:T(8,128)S(1)}, f32[48,192]{1,0:T(8,128)S(1)}, u32[]{:S(2)}, u32[]{:S(2)}) collective-permute-start(f32[48,192]{1,0:T(8,128)S(1)} %get-tuple-element.37), channel_id=1, source_target_pairs={{0,6},{1,7},{2,0},{3,1},{4,2},{5,3},{6,4},{7,5},{8,14},{9,15},{10,... | collective-permute-start | bytes 110600 | tf_op jit(solution)/shard_map/ppermute | solution.py:36
  41.7 1.5 %dynamic-slice_bitcast_fusion.1 = f32[1,1,64,256]{3,2,1,0:T(8,128)} fusion(f32[256,256]{1,0:T(8,128)} %copy-done.13, s32[]{:T(128)S(6)} %select_n.92), kind=kLoop, calls=%fused_computation.114 | loop fusion | bytes 131076 | tf_op jit(solution)/shard_map/broadcast_in_dim | solution.py:130
  43.2 1.1 %collective-permute-done.2 = f32[48,192]{1,0:T(8,128)S(1)} collective-permute-done((f32[48,192]{1,0:T(8,128)S(1)}, f32[48,192]{1,0:T(8,128)S(1)}, u32[]{:S(2)}, u32[]{:S(2)}) %collective-permute-start.2) | collective-permute-done | bytes 36896 | tf_op jit(solution)/shard_map/ppermute | solution.py:36
  44.2 0.4 collective-permute-done.3
  44.6 0.6 %fusion.67 = f32[1,48,192]{2,1,0:T(8,128)} fusion(f32[48,192]{1,0:T(8,128)S(1)} %collective-permute-done.3, f32[48,192]{1,0:T(8,128)S(1)} %collective-permute-done.2, f32[48,192]{1,0:T(8,128)S(1)} %collective-permute-done.1, f32[4,48,192]{2,1,0:T(8,128)S(1)} %bitcast_add_fusion, s32[]{:T(128)S(6)} %select_n.85), kind=kLoop, calls=%fused_computation.118 | loop fusion | flops 27648 | bytes 184324 | tf_op jit(solution)/shard_map/broadcast_in_dim | solution.py:130
  (33 shorter events, 0.3 us)
Async XLA Ops:
  0.6 22.9 %copy-start = (bf16[1,256,384]{2,1,0:T(8,128)(2,1)S(1)}, bf16[1,256,384]{2,1,0:T(8,128)(2,1)}, u32[]{:S(2)}) copy-start(bf16[1,256,384]{2,1,0:T(8,128)(2,1)} %param.12) | copy-start | bytes 589828
  0.6 1.5 %copy-start.11 = (bf16[1,384,768]{2,1,0:T(8,128)(2,1)S(1)}, bf16[1,384,768]{2,1,0:T(8,128)(2,1)}, u32[]{:S(2)}) copy-start(bf16[1,384,768]{2,1,0:T(8,128)(2,1)} %param.9) | copy-start | bytes 1769476
  0.7 1.8 %copy-start.12 = (f32[384,384]{1,0:T(8,128)S(1)}, f32[384,384]{1,0:T(8,128)}, u32[]{:S(2)}) copy-start(f32[384,384]{1,0:T(8,128)} %param.11) | copy-start | bytes 1769476
  2.2 1.1 %copy-start.1 = (bf16[384,768]{1,0:T(8,128)(2,1)S(1)}, bf16[384,768]{1,0:T(8,128)(2,1)}, u32[]{:S(2)}) copy-start(bf16[384,768]{1,0:T(8,128)(2,1)} %constant.113.clone) | copy-start | bytes 1769476
  2.2 1.1 %copy-start.14 = (bf16[1,128,384]{2,1,0:T(8,128)(2,1)S(1)}, bf16[1,128,384]{2,1,0:T(8,128)(2,1)}, u32[]{:S(2)}) copy-start(bf16[1,128,384]{2,1,0:T(8,128)(2,1)} %param.13) | copy-start | bytes 294916
  23.5 0.7 %copy-start.15 = (s32[1,256]{1,0:T(1,128)S(1)}, s32[1,256]{1,0:T(1,128)}, u32[]{:S(2)}) copy-start(s32[1,256]{1,0:T(1,128)} %param.15) | copy-start | bytes 3076
  26.7 0.9 %copy-start.16 = (bf16[1,1,256,256]{3,2,1,0:T(8,128)(2,1)S(1)}, bf16[1,1,256,256]{3,2,1,0:T(8,128)(2,1)}, u32[]{:S(2)}) copy-start(bf16[1,1,256,256]{3,2,1,0:T(8,128)(2,1)} %param.14) | copy-start | bytes 393220
  27.8 0.7 %copy-start.13 = (f32[256,256]{1,0:T(8,128)}, f32[256,256]{1,0:T(8,128)S(1)}, u32[]{:S(2)}) copy-start(f32[256,256]{1,0:T(8,128)S(1)} %fusion.4) | copy-start | bytes 786436
  29.3 1.8 %copy-start.10 = (f32[384,384]{0,1:T(8,128)S(1)}, f32[384,384]{0,1:T(8,128)}, u32[]{:S(2)}) copy-start(f32[384,384]{0,1:T(8,128)} %get-tuple-element.23) | copy-start | bytes 1769476
  29.8 1.4 %copy-start.7 = (f32[384,384]{0,1:T(8,128)S(1)}, f32[384,384]{0,1:T(8,128)}, u32[]{:S(2)}) copy-start(f32[384,384]{0,1:T(8,128)} %get-tuple-element.20) | copy-start | bytes 1769476
  29.8 1.4 %copy-start.8 = (f32[384,384]{0,1:T(8,128)S(1)}, f32[384,384]{0,1:T(8,128)}, u32[]{:S(2)}) copy-start(f32[384,384]{0,1:T(8,128)} %get-tuple-element.21) | copy-start | bytes 1769476
  29.8 1.4 %copy-start.9 = (f32[384,384]{0,1:T(8,128)S(1)}, f32[384,384]{0,1:T(8,128)}, u32[]{:S(2)}) copy-start(f32[384,384]{0,1:T(8,128)} %get-tuple-element.22) | copy-start | bytes 1769476
  30.2 1.3 %copy-start.4 = (f32[384,384]{0,1:T(8,128)S(1)}, f32[384,384]{0,1:T(8,128)}, u32[]{:S(2)}) copy-start(f32[384,384]{0,1:T(8,128)} %get-tuple-element.17) | copy-start | bytes 1769476
  30.3 1.4 %copy-start.5 = (f32[384,384]{0,1:T(8,128)S(1)}, f32[384,384]{0,1:T(8,128)}, u32[]{:S(2)}) copy-start(f32[384,384]{0,1:T(8,128)} %get-tuple-element.18) | copy-start | bytes 1769476
  30.3 1.6 %copy-start.6 = (f32[384,384]{0,1:T(8,128)S(1)}, f32[384,384]{0,1:T(8,128)}, u32[]{:S(2)}) copy-start(f32[384,384]{0,1:T(8,128)} %get-tuple-element.19) | copy-start | bytes 1769476
  30.7 1.4 %copy-start.2 = (f32[384,384]{0,1:T(8,128)S(1)}, f32[384,384]{0,1:T(8,128)}, u32[]{:S(2)}) copy-start(f32[384,384]{0,1:T(8,128)} %get-tuple-element.15) | copy-start | bytes 1769476
  30.7 1.6 %copy-start.3 = (f32[384,384]{0,1:T(8,128)S(1)}, f32[384,384]{0,1:T(8,128)}, u32[]{:S(2)}) copy-start(f32[384,384]{0,1:T(8,128)} %get-tuple-element.16) | copy-start | bytes 1769476
  33.1 1.6 %collective-permute-start = (f32[4,48,192]{2,1,0:T(8,128)S(1)}, f32[4,48,192]{2,1,0:T(8,128)S(1)}, u32[]{:S(2)}, u32[]{:S(2)}) collective-permute-start(f32[4,48,192]{2,1,0:T(8,128)S(1)} %dynamic-slice_bitcast_fusion), channel_id=1, source_target_pairs={{0,1},{1,0},{2,3},{3,2},{4,5},{5,4},{6,7},{7,6},{8,9},{9,8},{10,11... | collective-permute-start | bytes 442376 | tf_op jit(solution)/shard_map/ppermute | solution.py:32
  34.8 8.4 %collective-permute-start.1 = (f32[48,192]{1,0:T(8,128)S(1)}, f32[48,192]{1,0:T(8,128)S(1)}, u32[]{:S(2)}, u32[]{:S(2)}) collective-permute-start(f32[48,192]{1,0:T(8,128)S(1)} %get-tuple-element.36), channel_id=1, source_target_pairs={{0,2},{1,3},{2,4},{3,5},{4,6},{5,7},{6,0},{7,1},{8,10},{9,11},{10,... | collective-permute-start | bytes 110600 | tf_op jit(solution)/shard_map/ppermute | solution.py:36
  37.8 6.5 %collective-permute-start.2 = (f32[48,192]{1,0:T(8,128)S(1)}, f32[48,192]{1,0:T(8,128)S(1)}, u32[]{:S(2)}, u32[]{:S(2)}) collective-permute-start(f32[48,192]{1,0:T(8,128)S(1)} %get-tuple-element.38), channel_id=1, source_target_pairs={{0,4},{1,5},{2,6},{3,7},{4,0},{5,1},{6,2},{7,3},{8,12},{9,13},{10,... | collective-permute-start | bytes 110600 | tf_op jit(solution)/shard_map/ppermute | solution.py:36
  40.4 4.2 %collective-permute-start.3 = (f32[48,192]{1,0:T(8,128)S(1)}, f32[48,192]{1,0:T(8,128)S(1)}, u32[]{:S(2)}, u32[]{:S(2)}) collective-permute-start(f32[48,192]{1,0:T(8,128)S(1)} %get-tuple-element.37), channel_id=1, source_target_pairs={{0,6},{1,7},{2,0},{3,1},{4,2},{5,3},{6,4},{7,5},{8,14},{9,15},{10,... | collective-permute-start | bytes 110600 | tf_op jit(solution)/shard_map/ppermute | solution.py:36

commit v2 on v1

v2 whole, which is shorter than its diff:
```python
import functools
import math

import jax
import jax.numpy as jnp
import numpy as np
from jax import lax
from jax.experimental import pallas as pl
from jax.experimental.pallas import tpu as pltpu
from jax.sharding import PartitionSpec as P

SUBSTEPS = 4
LANES = 128
WINDOW = 256
CHUNK = 128


def dft_tables(length):
    wrapped = np.outer(np.arange(length), np.arange(length)) % length
    angles = wrapped * (2.0 * math.pi / length)
    factor = 1.0 / math.sqrt(length)
    return np.concatenate([np.cos(angles) * factor, -np.sin(angles) * factor], 1)


def dot(a, b, contract=((1,), (0,))):
    return lax.dot_general(a, b, (contract, ((), ())), preferred_element_type=jnp.float32)


def sine_cosine(x):
    y = x * x
    sine = -1.0 / math.factorial(11)
    for power in (9, 7, 5, 3):
        sine = sine * y + (-1.0) ** (power // 2) / math.factorial(power)
    sine = x * (sine * y + 1.0)
    cosine = 1.0 / math.factorial(12)
    for power in (10, 8, 6, 4, 2):
        cosine = cosine * y + (-1.0) ** (power // 2) / math.factorial(power)
    return sine, cosine * y + 1.0


def local_kernel(
    seg_total,
    coil_total,
    packed,
    count_ref,
    time_ref,
    rows_hbm,
    fourier_hbm,
    cols_hbm,
    field_hbm,
    maps_hbm,
    image_hbm,
    measured_hbm,
    term_ref,
    own_ref,
    rows_ref,
    fourier_ref,
    cols_ref,
    field_ref,
    maps_ref,
    image_ref,
    measured_ref,
    wave_ref,
    phase_ref,
    left_ref,
    right_ref,
    misfit_ref,
    adjoint_ref,
    turned_ref,
    sems,
):
    pixels = field_ref.shape[0]
    row_total = rows_ref.shape[0]
    col_total = cols_ref.shape[0]
    own_rows = row_total // seg_total
    width = 2 * pixels // seg_total
    pairs = seg_total // 2
    block_rows = pixels // coil_total
    segment = lax.axis_index("seg")
    member = lax.axis_index("coil")

    copies = [
        pltpu.make_async_copy(source, target, sems.at[i])
        for i, (source, target) in enumerate(
            (
                (rows_hbm, rows_ref),
                (fourier_hbm, fourier_ref),
                (cols_hbm, cols_ref),
                (field_hbm, field_ref),
                (maps_hbm, maps_ref),
                (image_hbm, image_ref),
                (measured_hbm, measured_ref),
            )
        )
    ]
    for copy in copies:
        copy.start()
    for copy in copies[:3]:
        copy.wait()

    grid_rows = rows_ref[...]
    grid_cols = cols_ref[...]
    fourier = fourier_ref[...]
    row_op = dot(grid_rows, fourier).astype(jnp.bfloat16)
    for part in range(2):
        span = slice(part * pixels, (part + 1) * pixels)
        adjoint_ref[:, part * row_total : (part + 1) * row_total] = dot(
            fourier[:, span], grid_rows, ((1,), (1,))
        ).astype(jnp.bfloat16)
    col_op = dot(grid_cols, fourier).astype(jnp.bfloat16)
    left_ref[:col_total, :pixels] = col_op[:, :pixels]
    left_ref[:col_total, pixels:] = -col_op[:, pixels:]
    left_ref[col_total:, :pixels] = col_op[:, pixels:]
    left_ref[col_total:, pixels:] = col_op[:, :pixels]
    col_re = dot(fourier[:, :pixels], grid_cols, ((1,), (1,))).astype(jnp.bfloat16)
    col_im = dot(fourier[:, pixels:], grid_cols, ((1,), (1,))).astype(jnp.bfloat16)
    right_ref[:pixels, :col_total] = col_re
    right_ref[:pixels, col_total:] = col_im
    right_ref[pixels:, :col_total] = -col_im
    right_ref[pixels:, col_total:] = col_re

    steps = jnp.broadcast_to(time_ref[...].astype(jnp.float32), (8, row_total))
    def weight(s):
        return jnp.maximum(0.0, 1.0 - jnp.abs(steps - float(s * SUBSTEPS)) / SUBSTEPS)
    along = []
    for pair in range(pairs):
        above, below = weight(pairs + pair), weight(pairs - 1 - pair)
        along += [above + below, above - below]

    for copy in copies[3:6]:
        copy.wait()
    right = right_ref[...]
    samples = None
    contracted = [[] for _ in range(seg_total)]
    for top in range(0, pixels, CHUNK):
        rows = slice(top, top + CHUNK)
        sine, cosine = sine_cosine(0.5 * field_ref[rows, :])
        image_re = image_ref[rows, :pixels].astype(jnp.float32)
        image_im = image_ref[rows, pixels:].astype(jnp.float32)
        map_re = maps_ref[rows, :pixels].astype(jnp.float32)
        map_im = maps_ref[rows, pixels:].astype(jnp.float32)
        base_re = image_re * map_re - image_im * map_im
        base_im = image_re * map_im + image_im * map_re
        twice_re = cosine * cosine - sine * sine
        twice_im = 2.0 * cosine * sine
        for pair in range(pairs):
            if pair:
                cosine, sine = (
                    cosine * twice_re - sine * twice_im,
                    cosine * twice_im + sine * twice_re,
                )
            phase_ref[2 * pair, rows, :] = cosine
            phase_ref[2 * pair + 1, rows, :] = sine
            wave_ref[2 * pair, rows, :pixels] = (base_re * cosine).astype(jnp.bfloat16)
            wave_ref[2 * pair, rows, pixels:] = (base_im * cosine).astype(jnp.bfloat16)
            wave_ref[2 * pair + 1, rows, :pixels] = (-base_im * sine).astype(jnp.bfloat16)
            wave_ref[2 * pair + 1, rows, pixels:] = (base_re * sine).astype(jnp.bfloat16)
        for i in range(seg_total):
            contracted[i].append(dot(wave_ref[i, rows, :], right).astype(jnp.bfloat16))
    for i in range(seg_total):
        v = jnp.concatenate(contracted[i], 0)
        turned = jnp.concatenate([-v[:, col_total:], v[:, :col_total]], 1)
        y = dot(row_op[:, :pixels], v) + dot(row_op[:, pixels:], turned)
        y = y * jnp.transpose(along[i])[:, :1]
        samples = y if samples is None else samples + y

    copies[6].wait()
    row_ids = lax.broadcasted_iota(jnp.int32, (row_total, 2 * col_total), 0)
    misfit = samples - measured_ref[...].astype(jnp.float32)
    misfit = jnp.where(row_ids < count_ref[0], misfit, 0.0)
    misfit_ref[...] = misfit
    own_start = pl.multiple_of(segment * own_rows, own_rows)
    own_copy = pltpu.make_async_copy(misfit_ref.at[pl.ds(own_start, own_rows)], own_ref, sems.at[7])
    own_copy.start()

    column = lax.rem(segment * width, pixels)
    imaginary = segment * width >= pixels
    start = jnp.minimum(column // LANES * LANES, pixels - WINDOW)
    start = pl.multiple_of(start, LANES)
    shift = column - start
    part_re = left_ref[:, pl.ds(start, WINDOW)]
    part_im = left_ref[:, pl.ds(pl.multiple_of(start + pixels, LANES), WINDOW)]
    misfit = misfit.astype(jnp.bfloat16)
    turn_re = dot(misfit, part_re).astype(jnp.bfloat16)
    turn_im = dot(misfit, part_im).astype(jnp.bfloat16)
    turned_ref[:row_total, :WINDOW] = turn_re
    turned_ref[:row_total, WINDOW:] = turn_im
    turned_ref[row_total:, :WINDOW] = turn_im
    turned_ref[row_total:, WINDOW:] = -turn_re
    turned = turned_ref[...]
    factor = coil_total ** (-0.5)
    for top in range(0, pixels, CHUNK):
        rows = slice(top, top + CHUNK)
        adjoint = adjoint_ref[rows, :]
        sum_re = None
        for pair in range(pairs):
            cosine = phase_ref[2 * pair, rows, pl.ds(start, WINDOW)]
            sine = phase_ref[2 * pair + 1, rows, pl.ds(start, WINDOW)]
            scale = [
                jnp.concatenate([along[2 * pair + i][:1]] * 2, 1).astype(jnp.bfloat16)
                for i in range(2)
            ]
            even = dot(adjoint * scale[0], turned)
            odd = dot(adjoint * scale[1], turned)
            add_re = cosine * even[:, :WINDOW] + sine * odd[:, WINDOW:]
            add_im = cosine * even[:, WINDOW:] - sine * odd[:, :WINDOW]
            sum_re = add_re if sum_re is None else sum_re + add_re
            sum_im = add_im if pair == 0 else sum_im + add_im
        map_re = maps_ref[rows, pl.ds(start, WINDOW)].astype(jnp.float32)
        map_im = maps_ref[rows, pl.ds(pl.multiple_of(start + pixels, LANES), WINDOW)].astype(
            jnp.float32
        )
        first = jnp.where(imaginary, -map_im, map_re) * factor
        second = jnp.where(imaginary, map_re, map_im) * factor
        term = first * sum_re + second * sum_im
        term = pltpu.roll(term, lax.rem(WINDOW - shift, WINDOW), 1)
        term_ref[rows, :] = term[:, :width]
    own_copy.wait()


def local_terms(seg_total, coil_total, image, maps, field, rows, cols, measured, time, count):
    pixels = field.shape[0]
    row_total, col_total = rows.shape[0], cols.shape[0]
    width = 2 * pixels // seg_total
    fourier = jnp.asarray(dft_tables(pixels), jnp.bfloat16)
    anywhere = pl.BlockSpec(memory_space=pl.ANY)
    vmem = pl.BlockSpec(memory_space=pltpu.VMEM)
    smem = pl.BlockSpec(memory_space=pltpu.SMEM)
    operands = (rows, fourier, cols, field, maps, image, measured)
    return pl.pallas_call(
        functools.partial(local_kernel, seg_total, coil_total, False),
        out_shape=(
            jax.ShapeDtypeStruct((pixels, width), jnp.float32),
            jax.ShapeDtypeStruct((row_total // seg_total, 2 * col_total), jnp.float32),
        ),
        in_specs=[smem, vmem] + [anywhere] * len(operands),
        out_specs=(vmem, anywhere),
        scratch_shapes=[pltpu.VMEM(x.shape, x.dtype) for x in operands]
        + [
            pltpu.VMEM((seg_total, pixels, 2 * pixels), jnp.bfloat16),
            pltpu.VMEM((seg_total, pixels, pixels), jnp.float32),
            pltpu.VMEM((2 * col_total, 2 * pixels), jnp.bfloat16),
            pltpu.VMEM((2 * pixels, 2 * col_total), jnp.bfloat16),
            pltpu.VMEM((row_total, 2 * col_total), jnp.float32),
            pltpu.VMEM((pixels, 2 * row_total), jnp.bfloat16),
            pltpu.VMEM((2 * row_total, 2 * WINDOW), jnp.bfloat16),
            pltpu.SemaphoreType.DMA((8,)),
        ],
        compiler_params=pltpu.CompilerParams(vmem_limit_bytes=56 * 1024 * 1024),
        name="local_terms",
    )(count, time, *operands)


def exchange_sum(blocks, axis):
    total = lax.axis_size(axis)
    me = lax.axis_index(axis)
    lane = me % 2
    group = me // 2
    groups = total // 2
    split = blocks.reshape(groups, 2, *blocks.shape[1:])
    away = lax.dynamic_index_in_dim(split, 1 - lane, 1, False)
    kept = lax.dynamic_index_in_dim(split, lane, 1, False)
    paired = kept + lax.ppermute(away, axis, [(i, i ^ 1) for i in range(total)])
    result = lax.dynamic_index_in_dim(paired, group, 0, False)
    for step in range(1, groups):
        piece = lax.dynamic_index_in_dim(paired, (group + step) % groups, 0, False)
        result = result + lax.ppermute(
            piece, axis, [(i, (i + 2 * step) % total) for i in range(total)]
        )
    return result


def shards(
    image_estimate,
    coil_maps,
    field_map,
    interp_rows,
    interp_cols,
    measured,
    sample_time,
    sample_count,
):
    seg_total = lax.axis_size("seg")
    coil_total = lax.axis_size("coil")
    pixels = field_map.shape[0]
    term, own = local_terms(
        seg_total,
        coil_total,
        image_estimate[0],
        coil_maps[0],
        field_map,
        interp_rows[0],
        interp_cols[0],
        measured[0, 0],
        sample_time,
        sample_count,
    )
    blocks = term.reshape(coil_total, pixels // coil_total, term.shape[1])
    gradient = exchange_sum(blocks, "coil")
    return gradient[None], own[None, None]


def solution(mesh):
    in_specs = (P(), P("coil", None, None), P(), P(), P(), P("coil", None, None, None), P(), P())
    out_specs = (P(None, "coil", "seg"), P("coil", None, "seg", None))
    return jax.shard_map(shards, mesh=mesh, in_specs=in_specs, out_specs=out_specs, check_vma=False)
```

time: 45.5 us -> 22.2 us (0.49)
  other arithmetic: 21.3 us -> 0.66 us
  Pallas kernels: 0 us -> 7.18 us
  local copies, waits for them, and re-layouts: 6.94 us -> 1.03 us
  matrix products: 5.23 us -> 0 us
  waiting for transfers between devices: 2.5 us -> 5.26 us
  starting transfers between devices: 7.48 us -> 6.58 us
    another operation x3 -> x0, other arithmetic: 19.6 us -> none
    pallas_call x0 -> x1, Pallas kernels: none -> 7.18 us  [local_terms(): pl.pallas_call(functools.partial(local_kernel, seg_total, coil_total, Fal...]
    dot_general x15 -> x0, matrix products: 5.23 us -> none  [the longest x7 2.05 us: dot(): return jnp.dot(a, b, preferred_element_type=jnp.float32)]
    unnamed x37 -> x2, local copies, waits for them, and re-layouts: 5.22 us -> 0.01 us
    ppermute x3, waiting for transfers between devices: 1.43 us -> 4.19 us  [exchange_sum(): lax.ppermute(piece, axis, [(i, (i + 2 * step) % total) for i in range(tot...]
    broadcast_in_dim x1 -> x0, local copies, waits for them, and re-layouts: 1.47 us -> none  [shards(): return (gradient[None], own[None, None])]
    squeeze x1, local copies, waits for them, and re-layouts: 0.02 us -> 1.01 us  [exchange_sum(): away = lax.dynamic_index_in_dim(split, 1 - lane, 1, False)]
    ppermute x3, starting transfers between devices: 6.92 us -> 6.02 us  [exchange_sum(): lax.ppermute(piece, axis, [(i, (i + 2 * step) % total) for i in range(tot...]
  transfers between devices with their start and end apart: 4 -> 4, of which waited for: 3 -> 4; matrix products, arithmetic and copies ran while one was open for 3% -> 0% of each run, Pallas kernels for 0% -> 0%
where the time goes in v2:
time: 22.2 us; the launch traced here: 22 us
  Pallas kernels  7.18 us (32%)
  starting transfers between devices  6.58 us (30%)
  waiting for transfers between devices  5.26 us (24%)
  between operations  1.33 us (6%)
  local copies, waits for them, and re-layouts  1.03 us (5%)
  other arithmetic  0.66 us (3%)
    pallas_call x1, Pallas kernels, local_terms(): pl.pallas_call(functools.partial(local_kernel, seg_total, coil_total, Fal...  7.18 us
    ppermute x3, starting transfers between devices, exchange_sum(): lax.ppermute(piece, axis, [(i, (i + 2 * step) % total) for i in range(tot...  6.02 us
    ppermute x3, waiting for transfers between devices, exchange_sum(): lax.ppermute(piece, axis, [(i, (i + 2 * step) % total) for i in range(tot...  4.19 us
    ppermute x1, waiting for transfers between devices, exchange_sum(): paired = kept + lax.ppermute(away, axis, [(i, i ^ 1) for i in range(total)])  1.07 us
    squeeze x1, local copies, waits for them, and re-layouts, exchange_sum(): away = lax.dynamic_index_in_dim(split, 1 - lane, 1, False)  1.01 us
    broadcast_in_dim x1, other arithmetic, shards(): return (gradient[None], own[None, None])  0.63 us
    ppermute x1, starting transfers between devices, exchange_sum(): paired = kept + lax.ppermute(away, axis, [(i, i ^ 1) for i in range(total)])  0.56 us
  transfers between devices with their start and end apart: 4, of which 4 were waited for; matrix products, arithmetic and copies ran while one was open for 0% of the time, Pallas kernels for 0%

profile of v2, /device:TPU:0, one launch (start us, length us, event | category | flops | bytes accessed | tf_op | source)
XLA Modules:
  0.0 22.0 jit_solution(5400431864591813126)
XLA Ops:
  1.3 7.2 %local_terms.1 = (f32[384,192]{1,0:T(8,128)}, f32[64,256]{1,0:T(8,128)}) custom-call(s32[1]{0:T(128)S(6)} %copy.11.count_ref, s32[1,256]{1,0:T(1,128)} %time_ref.1, bf16[256,384]{1,0:T(8,128)(2,1)} %bitcast.31, bf16[384,768]{1,0:T(8,128)(2,1)} %constant.67.clone.fourier_hbm, bf16[128,384]{1,0:T(8,128)(2,1)} %bitcast.33, f32[384,384]{1,0:T(8,128)} %field_hbm.1, ...), custom_call_target="tpu_custom_call" | custom-call | tf_op jit(solution)/shard_map/local_terms/pallas_call | solution.py:230
  8.5 0.0 copy-start
  8.5 1.0 %dynamic-slice_bitcast_fusion = f32[4,48,192]{2,1,0:T(8,128)S(1)} fusion(f32[4,2,48,192]{3,2,1,0:T(8,128)} %bitcast.29, s32[]{:T(128)S(6)} %select_n.45), kind=kLoop, calls=%fused_computation.1 | loop fusion | bytes 294916 | tf_op jit(solution)/shard_map/jit(dynamic_index_in_dim)/squeeze | solution.py:261
  9.5 0.6 %collective-permute-start = (f32[4,48,192]{2,1,0:T(8,128)S(1)}, f32[4,48,192]{2,1,0:T(8,128)S(1)}, u32[]{:S(2)}, u32[]{:S(2)}) collective-permute-start(f32[4,48,192]{2,1,0:T(8,128)S(1)} %dynamic-slice_bitcast_fusion), channel_id=1, source_target_pairs={{0,1},{1,0},{2,3},{3,2},{4,5},{5,4},{6,7},{7,6},{8,9},{9,8},{10,11... | collective-permute-start | bytes 442376 | tf_op jit(solution)/shard_map/ppermute | solution.py:263
  10.1 1.1 %collective-permute-done = f32[4,48,192]{2,1,0:T(8,128)S(1)} collective-permute-done((f32[4,48,192]{2,1,0:T(8,128)S(1)}, f32[4,48,192]{2,1,0:T(8,128)S(1)}, u32[]{:S(2)}, u32[]{:S(2)}) %collective-permute-start) | collective-permute-done | bytes 147488 | tf_op jit(solution)/shard_map/ppermute | solution.py:263
  11.1 0.0 copy-done
  11.2 3.0 %collective-permute-start.1 = (f32[48,192]{1,0:T(8,128)S(1)}, f32[48,192]{1,0:T(8,128)S(1)}, u32[]{:S(2)}, u32[]{:S(2)}) collective-permute-start(f32[48,192]{1,0:T(8,128)S(1)} %get-tuple-element.6), channel_id=1, source_target_pairs={{0,2},{1,3},{2,4},{3,5},{4,6},{5,7},{6,0},{7,1},{8,10},{9,11},{10,... | collective-permute-start | bytes 110600 | tf_op jit(solution)/shard_map/ppermute | solution.py:267
  14.2 2.1 %collective-permute-start.3 = (f32[48,192]{1,0:T(8,128)S(1)}, f32[48,192]{1,0:T(8,128)S(1)}, u32[]{:S(2)}, u32[]{:S(2)}) collective-permute-start(f32[48,192]{1,0:T(8,128)S(1)} %get-tuple-element.7), channel_id=1, source_target_pairs={{0,6},{1,7},{2,0},{3,1},{4,2},{5,3},{6,4},{7,5},{8,14},{9,15},{10,... | collective-permute-start | bytes 110600 | tf_op jit(solution)/shard_map/ppermute | solution.py:267
  16.3 0.9 %collective-permute-start.2 = (f32[48,192]{1,0:T(8,128)S(1)}, f32[48,192]{1,0:T(8,128)S(1)}, u32[]{:S(2)}, u32[]{:S(2)}) collective-permute-start(f32[48,192]{1,0:T(8,128)S(1)} %get-tuple-element.8), channel_id=1, source_target_pairs={{0,4},{1,5},{2,6},{3,7},{4,0},{5,1},{6,2},{7,3},{8,12},{9,13},{10,... | collective-permute-start | bytes 110600 | tf_op jit(solution)/shard_map/ppermute | solution.py:267
  17.2 1.1 %collective-permute-done.1 = f32[48,192]{1,0:T(8,128)S(1)} collective-permute-done((f32[48,192]{1,0:T(8,128)S(1)}, f32[48,192]{1,0:T(8,128)S(1)}, u32[]{:S(2)}, u32[]{:S(2)}) %collective-permute-start.1) | collective-permute-done | bytes 36896 | tf_op jit(solution)/shard_map/ppermute | solution.py:267
  18.3 0.5 %collective-permute-done.3 = f32[48,192]{1,0:T(8,128)S(1)} collective-permute-done((f32[48,192]{1,0:T(8,128)S(1)}, f32[48,192]{1,0:T(8,128)S(1)}, u32[]{:S(2)}, u32[]{:S(2)}) %collective-permute-start.3) | collective-permute-done | bytes 36896 | tf_op jit(solution)/shard_map/ppermute | solution.py:267
  18.8 2.6 %collective-permute-done.2 = f32[48,192]{1,0:T(8,128)S(1)} collective-permute-done((f32[48,192]{1,0:T(8,128)S(1)}, f32[48,192]{1,0:T(8,128)S(1)}, u32[]{:S(2)}, u32[]{:S(2)}) %collective-permute-start.2) | collective-permute-done | bytes 36896 | tf_op jit(solution)/shard_map/ppermute | solution.py:267
  21.4 0.6 %fusion.2 = f32[1,48,192]{2,1,0:T(8,128)} fusion(f32[48,192]{1,0:T(8,128)S(1)} %collective-permute-done.3, f32[48,192]{1,0:T(8,128)S(1)} %collective-permute-done.2, f32[48,192]{1,0:T(8,128)S(1)} %collective-permute-done.1, f32[4,48,192]{2,1,0:T(8,128)S(1)} %bitcast_add_fusion, s32[]{:T(128)S(6)} %select_n.47), kind=kLoop, calls=%fused_computation.5 | loop fusion | flops 27648 | bytes 184324 | tf_op jit(solution)/shard_map/broadcast_in_dim | solution.py:300
  (2 shorter events, 0.0 us)
Async XLA Ops:
  8.5 2.7 %copy-start = (f32[384,192]{1,0:T(8,128)S(1)}, f32[384,192]{1,0:T(8,128)}, u32[]{:S(2)}) copy-start(f32[384,192]{1,0:T(8,128)} %get-tuple-element.4) | copy-start | bytes 884740
  9.5 1.6 %collective-permute-start = (f32[4,48,192]{2,1,0:T(8,128)S(1)}, f32[4,48,192]{2,1,0:T(8,128)S(1)}, u32[]{:S(2)}, u32[]{:S(2)}) collective-permute-start(f32[4,48,192]{2,1,0:T(8,128)S(1)} %dynamic-slice_bitcast_fusion), channel_id=1, source_target_pairs={{0,1},{1,0},{2,3},{3,2},{4,5},{5,4},{6,7},{7,6},{8,9},{9,8},{10,11... | collective-permute-start | bytes 442376 | tf_op jit(solution)/shard_map/ppermute | solution.py:263
  11.2 7.1 %collective-permute-start.1 = (f32[48,192]{1,0:T(8,128)S(1)}, f32[48,192]{1,0:T(8,128)S(1)}, u32[]{:S(2)}, u32[]{:S(2)}) collective-permute-start(f32[48,192]{1,0:T(8,128)S(1)} %get-tuple-element.6), channel_id=1, source_target_pairs={{0,2},{1,3},{2,4},{3,5},{4,6},{5,7},{6,0},{7,1},{8,10},{9,11},{10,... | collective-permute-start | bytes 110600 | tf_op jit(solution)/shard_map/ppermute | solution.py:267
  14.2 4.6 %collective-permute-start.3 = (f32[48,192]{1,0:T(8,128)S(1)}, f32[48,192]{1,0:T(8,128)S(1)}, u32[]{:S(2)}, u32[]{:S(2)}) collective-permute-start(f32[48,192]{1,0:T(8,128)S(1)} %get-tuple-element.7), channel_id=1, source_target_pairs={{0,6},{1,7},{2,0},{3,1},{4,2},{5,3},{6,4},{7,5},{8,14},{9,15},{10,... | collective-permute-start | bytes 110600 | tf_op jit(solution)/shard_map/ppermute | solution.py:267
  16.3 5.1 %collective-permute-start.2 = (f32[48,192]{1,0:T(8,128)S(1)}, f32[48,192]{1,0:T(8,128)S(1)}, u32[]{:S(2)}, u32[]{:S(2)}) collective-permute-start(f32[48,192]{1,0:T(8,128)S(1)} %get-tuple-element.8), channel_id=1, source_target_pairs={{0,4},{1,5},{2,6},{3,7},{4,0},{5,1},{6,2},{7,3},{8,12},{9,13},{10,... | collective-permute-start | bytes 110600 | tf_op jit(solution)/shard_map/ppermute | solution.py:267

commit v3 on v2

v3 whole, which is shorter than its diff:
```python
import functools
import math

import jax
import jax.numpy as jnp
import numpy as np
from jax import lax
from jax.experimental import pallas as pl
from jax.experimental.pallas import tpu as pltpu
from jax.sharding import PartitionSpec as P

SUBSTEPS = 4
LANES = 128
WINDOW = 256
CHUNK = 128
PIECE = 16
TALL = 48


def dft_tables(length):
    wrapped = np.outer(np.arange(length), np.arange(length)) % length
    angles = wrapped * (2.0 * math.pi / length)
    factor = 1.0 / math.sqrt(length)
    return np.concatenate([np.cos(angles) * factor, -np.sin(angles) * factor], 1)


def dot(a, b, contract=((1,), (0,))):
    return lax.dot_general(a, b, (contract, ((), ())), preferred_element_type=jnp.float32)


def sine_cosine(x):
    y = x * x
    sine = -1.0 / math.factorial(11)
    for power in (9, 7, 5, 3):
        sine = sine * y + (-1.0) ** (power // 2) / math.factorial(power)
    sine = x * (sine * y + 1.0)
    cosine = 1.0 / math.factorial(12)
    for power in (10, 8, 6, 4, 2):
        cosine = cosine * y + (-1.0) ** (power // 2) / math.factorial(power)
    return sine, cosine * y + 1.0


def pack(block):
    rows, width = block.shape
    if not packs(rows, width):
        return (block,)
    full = width - LANES // 2
    tail = jnp.concatenate([block[: rows // 2, full:], block[rows // 2 :, full:]], 1)
    return tuple(block[:, i : i + LANES] for i in range(0, full, LANES)) + (tail,)


def packs(rows, width):
    return width > LANES and width % LANES == LANES // 2 and rows % 16 == 0


def packed_shape(rows, width):
    return (rows * width // LANES, LANES) if packs(rows, width) else (rows, width)


def unpack(block, rows, width):
    if not packs(rows, width):
        return block
    full = width - LANES // 2
    count = full // LANES
    pieces = [block[i * rows : (i + 1) * rows] for i in range(count)]
    tail = block[count * rows :]
    pieces.append(jnp.concatenate([tail[:, : LANES // 2], tail[:, LANES // 2 :]], 0))
    return jnp.concatenate(pieces, 1)


def local_kernel(
    seg_total,
    coil_total,
    count_hbm,
    time_hbm,
    rows_hbm,
    fourier_hbm,
    cols_hbm,
    field_hbm,
    maps_hbm,
    image_hbm,
    measured_hbm,
    kept_ref,
    away_ref,
    own_ref,
    count_ref,
    time_ref,
    rows_ref,
    fourier_ref,
    cols_ref,
    field_ref,
    maps_ref,
    image_ref,
    measured_ref,
    wave_ref,
    phase_ref,
    left_ref,
    right_ref,
    inner_ref,
    misfit_ref,
    adjoint_ref,
    turned_ref,
    scaled_ref,
    back_ref,
    term_ref,
    sems,
):
    pixels = field_ref.shape[0]
    row_total = rows_ref.shape[0]
    col_total = cols_ref.shape[0]
    own_rows = row_total // seg_total
    width = 2 * pixels // seg_total
    pairs = seg_total // 2
    block_rows = pixels // coil_total
    groups = coil_total // 2
    segment = lax.axis_index("seg")
    member = lax.axis_index("coil")

    copies = [
        pltpu.make_async_copy(source, target, sems.at[i])
        for i, (source, target) in enumerate(
            (
                (rows_hbm, rows_ref),
                (fourier_hbm, fourier_ref),
                (cols_hbm, cols_ref),
                (time_hbm, time_ref),
                (field_hbm, field_ref),
                (maps_hbm, maps_ref),
                (image_hbm, image_ref),
                (measured_hbm, measured_ref),
                (count_hbm, count_ref),
            )
        )
    ]
    for copy in copies:
        copy.start()
    for copy in copies[:4]:
        copy.wait()

    grid_rows = rows_ref[...]
    grid_cols = cols_ref[...]
    fourier = fourier_ref[...]
    row_op = dot(grid_rows, fourier).astype(jnp.bfloat16)
    for part in range(2):
        span = slice(part * pixels, (part + 1) * pixels)
        adjoint_ref[:, part * row_total : (part + 1) * row_total] = dot(
            fourier[:, span], grid_rows, ((1,), (1,))
        ).astype(jnp.bfloat16)
    col_op = dot(grid_cols, fourier).astype(jnp.bfloat16)
    left_ref[:col_total, :pixels] = col_op[:, :pixels]
    left_ref[:col_total, pixels:] = -col_op[:, pixels:]
    left_ref[col_total:, :pixels] = col_op[:, pixels:]
    left_ref[col_total:, pixels:] = col_op[:, :pixels]
    col_re = dot(fourier[:, :pixels], grid_cols, ((1,), (1,))).astype(jnp.bfloat16)
    col_im = dot(fourier[:, pixels:], grid_cols, ((1,), (1,))).astype(jnp.bfloat16)
    right_ref[:pixels, :col_total] = col_re
    right_ref[:pixels, col_total:] = col_im
    right_ref[pixels:, :col_total] = -col_im
    right_ref[pixels:, col_total:] = col_re

    steps = jnp.broadcast_to(time_ref[...].astype(jnp.float32), (8, row_total))

    def weight(s):
        return jnp.maximum(0.0, 1.0 - jnp.abs(steps - float(s * SUBSTEPS)) / SUBSTEPS)

    along = []
    for pair in range(pairs):
        above, below = weight(pairs + pair), weight(pairs - 1 - pair)
        along += [above + below, above - below]
    adjoint = adjoint_ref[...]
    for i in range(seg_total):
        scale = jnp.concatenate([along[i][:1]] * 2, 1).astype(jnp.bfloat16)
        scaled_ref[i] = adjoint * scale

    for copy in copies[4:7]:
        copy.wait()
    right = right_ref[...]
    for chunk in range(pixels // CHUNK):
        for low in range(0, CHUNK, PIECE):
            rows = slice(chunk * CHUNK + low, chunk * CHUNK + low + PIECE)
            sine, cosine = sine_cosine(0.5 * field_ref[rows, :])
            image_re = image_ref[rows, :pixels].astype(jnp.float32)
            image_im = image_ref[rows, pixels:].astype(jnp.float32)
            map_re = maps_ref[rows, :pixels].astype(jnp.float32)
            map_im = maps_ref[rows, pixels:].astype(jnp.float32)
            base_re = image_re * map_re - image_im * map_im
            base_im = image_re * map_im + image_im * map_re
            twice_re = cosine * cosine - sine * sine
            twice_im = 2.0 * cosine * sine
            for pair in range(pairs):
                if pair:
                    cosine, sine = (
                        cosine * twice_re - sine * twice_im,
                        cosine * twice_im + sine * twice_re,
                    )
                phase_ref[2 * pair, rows, :] = cosine
                phase_ref[2 * pair + 1, rows, :] = sine
                even = slice(2 * pair * CHUNK + low, 2 * pair * CHUNK + low + PIECE)
                odd = slice(even.start + CHUNK, even.stop + CHUNK)
                wave_ref[chunk, even, :pixels] = (base_re * cosine).astype(jnp.bfloat16)
                wave_ref[chunk, even, pixels:] = (base_im * cosine).astype(jnp.bfloat16)
                wave_ref[chunk, odd, :pixels] = (-base_im * sine).astype(jnp.bfloat16)
                wave_ref[chunk, odd, pixels:] = (base_re * sine).astype(jnp.bfloat16)
        v = dot(wave_ref[chunk], right).astype(jnp.bfloat16)
        for i in range(seg_total):
            piece = v[i * CHUNK : (i + 1) * CHUNK]
            first = slice(chunk * CHUNK, (chunk + 1) * CHUNK)
            second = slice(pixels + first.start, pixels + first.stop)
            inner_ref[i, first, :] = piece
            inner_ref[i, second, :col_total] = -piece[:, col_total:]
            inner_ref[i, second, col_total:] = piece[:, :col_total]
    samples = None
    for i in range(seg_total):
        y = dot(row_op, inner_ref[i]) * jnp.transpose(along[i])[:, :1]
        samples = y if samples is None else samples + y

    copies[7].wait()
    copies[8].wait()
    row_ids = lax.broadcasted_iota(jnp.int32, (row_total, 2 * col_total), 0)
    misfit = samples - measured_ref[...].astype(jnp.float32)
    misfit = jnp.where(row_ids < count_ref[0], misfit, 0.0)
    misfit_ref[...] = misfit
    own_start = pl.multiple_of(segment * own_rows, own_rows)
    own_copy = pltpu.make_async_copy(misfit_ref.at[pl.ds(own_start, own_rows)], own_ref, sems.at[9])
    own_copy.start()

    column = lax.rem(segment * width, pixels)
    imaginary = segment * width >= pixels
    start = jnp.minimum(column // LANES * LANES, pixels - WINDOW)
    start = pl.multiple_of(start, LANES)
    after = pl.multiple_of(start + pixels, LANES)
    shift = lax.rem(WINDOW - (column - start), WINDOW)
    misfit = misfit.astype(jnp.bfloat16)
    turn_re = dot(misfit, left_ref[:, pl.ds(start, WINDOW)]).astype(jnp.bfloat16)
    turn_im = dot(misfit, left_ref[:, pl.ds(after, WINDOW)]).astype(jnp.bfloat16)
    turned_ref[:row_total, :WINDOW] = turn_re
    turned_ref[:row_total, WINDOW:] = turn_im
    turned_ref[row_total:, :WINDOW] = turn_im
    turned_ref[row_total:, WINDOW:] = -turn_re
    turned = turned_ref[...]
    factor = coil_total ** (-0.5)
    for i in range(seg_total):
        back_ref[i] = dot(scaled_ref[i], turned)
    for low in range(0, pixels, TALL):
        rows = slice(low, low + TALL)
        sum_re = None
        for pair in range(pairs):
            cosine = phase_ref[2 * pair, rows, pl.ds(start, WINDOW)]
            sine = phase_ref[2 * pair + 1, rows, pl.ds(start, WINDOW)]
            add_re = cosine * back_ref[2 * pair, rows, :WINDOW]
            add_re = add_re + sine * back_ref[2 * pair + 1, rows, WINDOW:]
            add_im = cosine * back_ref[2 * pair, rows, WINDOW:]
            add_im = add_im - sine * back_ref[2 * pair + 1, rows, :WINDOW]
            sum_re = add_re if sum_re is None else sum_re + add_re
            sum_im = add_im if pair == 0 else sum_im + add_im
        map_re = maps_ref[rows, pl.ds(start, WINDOW)].astype(jnp.float32)
        map_im = maps_ref[rows, pl.ds(after, WINDOW)].astype(jnp.float32)
        first = jnp.where(imaginary, -map_im, map_re) * factor
        second = jnp.where(imaginary, map_re, map_im) * factor
        term_ref[rows, :] = pltpu.roll(first * sum_re + second * sum_im, shift, 1)

    lane = lax.rem(member, 2)
    group = member // 2
    for g in range(groups):
        slot = lax.rem(g + groups - group, groups)
        upper = term_ref[2 * g * block_rows : (2 * g + 1) * block_rows, :width]
        lower = term_ref[(2 * g + 1) * block_rows : (2 * g + 2) * block_rows, :width]
        for ref, value in (
            (kept_ref, jnp.where(lane == 0, upper, lower)),
            (away_ref, jnp.where(lane == 0, lower, upper)),
        ):
            top = 0
            for piece in pack(value):
                ref[slot, top : top + piece.shape[0], :] = piece
                top += piece.shape[0]
    own_copy.wait()


def local_terms(seg_total, coil_total, image, maps, field, rows, cols, measured, time, count):
    pixels = field.shape[0]
    row_total, col_total = rows.shape[0], cols.shape[0]
    width = 2 * pixels // seg_total
    fourier = jnp.asarray(dft_tables(pixels), jnp.bfloat16)
    anywhere = pl.BlockSpec(memory_space=pl.ANY)
    vmem = pl.BlockSpec(memory_space=pltpu.VMEM)
    operands = (time, rows, fourier, cols, field, maps, image, measured)
    blocks = (coil_total // 2, *packed_shape(pixels // coil_total, width))
    return pl.pallas_call(
        functools.partial(local_kernel, seg_total, coil_total),
        out_shape=(
            pltpu.VMEM(blocks, jnp.float32),
            pltpu.VMEM(blocks, jnp.float32),
            jax.ShapeDtypeStruct((row_total // seg_total, 2 * col_total), jnp.float32),
        ),
        in_specs=[anywhere] * (1 + len(operands)),
        out_specs=(vmem, vmem, anywhere),
        scratch_shapes=[pltpu.SMEM(count.shape, count.dtype)]
        + [pltpu.VMEM(x.shape, x.dtype) for x in operands]
        + [
            pltpu.VMEM((pixels // CHUNK, seg_total * CHUNK, 2 * pixels), jnp.bfloat16),
            pltpu.VMEM((seg_total, pixels, pixels), jnp.float32),
            pltpu.VMEM((2 * col_total, 2 * pixels), jnp.bfloat16),
            pltpu.VMEM((2 * pixels, 2 * col_total), jnp.bfloat16),
            pltpu.VMEM((seg_total, 2 * pixels, 2 * col_total), jnp.bfloat16),
            pltpu.VMEM((row_total, 2 * col_total), jnp.float32),
            pltpu.VMEM((pixels, 2 * row_total), jnp.bfloat16),
            pltpu.VMEM((2 * row_total, 2 * WINDOW), jnp.bfloat16),
            pltpu.VMEM((seg_total, pixels, 2 * row_total), jnp.bfloat16),
            pltpu.VMEM((seg_total, pixels, 2 * WINDOW), jnp.float32),
            pltpu.VMEM((pixels, WINDOW), jnp.float32),
            pltpu.SemaphoreType.DMA((10,)),
        ],
        compiler_params=pltpu.CompilerParams(vmem_limit_bytes=56 * 1024 * 1024),
        name="local_terms",
    )(count, *operands)


def exchange_sum(kept, away, axis):
    total = lax.axis_size(axis)
    paired = kept + lax.ppermute(away, axis, [(i, i ^ 1) for i in range(total)])
    result = paired[0]
    for step in range(1, total // 2):
        result = result + lax.ppermute(
            paired[step], axis, [(i, (i + 2 * step) % total) for i in range(total)]
        )
    return result


def shards(
    image_estimate,
    coil_maps,
    field_map,
    interp_rows,
    interp_cols,
    measured,
    sample_time,
    sample_count,
):
    seg_total = lax.axis_size("seg")
    coil_total = lax.axis_size("coil")
    pixels = field_map.shape[0]
    kept, away, own = local_terms(
        seg_total,
        coil_total,
        image_estimate[0],
        coil_maps[0],
        field_map,
        interp_rows[0],
        interp_cols[0],
        measured[0, 0],
        sample_time,
        sample_count,
    )
    total = exchange_sum(kept, away, "coil")
    gradient = unpack(total, pixels // coil_total, 2 * pixels // seg_total)
    return gradient[None], own[None, None]


def solution(mesh):
    in_specs = (P(), P("coil", None, None), P(), P(), P(), P("coil", None, None, None), P(), P())
    out_specs = (P(None, "coil", "seg"), P("coil", None, "seg", None))
    return jax.shard_map(shards, mesh=mesh, in_specs=in_specs, out_specs=out_specs, check_vma=False)
```

time: 22.2 us -> 20.3 us (0.914)
  local copies, waits for them, and re-layouts: 1.03 us -> 0.09 us
  Pallas kernels: 7.18 us -> 6.63 us
  waiting for transfers between devices: 5.26 us -> 4.92 us
    squeeze x2 -> x1, local copies, waits for them, and re-layouts: 1.03 us -> 0.01 us  [exchange_sum(): paired[step]]
    pallas_call x1, Pallas kernels: 7.18 us -> 6.63 us  [local_terms(): pl.pallas_call(functools.partial(local_kernel, seg_total, coil_total), ou...]
    ppermute x3, waiting for transfers between devices: 4.19 us -> 3.91 us  [exchange_sum(): lax.ppermute(paired[step], axis, [(i, (i + 2 * step) % total) for i in ra...]
where the time goes in v3:
time: 20.3 us; the launch traced here: 20.2 us
  Pallas kernels  6.63 us (33%)
  starting transfers between devices  6.57 us (32%)
  waiting for transfers between devices  4.92 us (24%)
  between operations  1.31 us (6%)
  other arithmetic  0.66 us (3%)
    pallas_call x1, Pallas kernels, local_terms(): pl.pallas_call(functools.partial(local_kernel, seg_total, coil_total), ou...  6.63 us
    ppermute x3, starting transfers between devices, exchange_sum(): lax.ppermute(paired[step], axis, [(i, (i + 2 * step) % total) for i in ra...  6.01 us
    ppermute x3, waiting for transfers between devices, exchange_sum(): lax.ppermute(paired[step], axis, [(i, (i + 2 * step) % total) for i in ra...  3.91 us
    ppermute x1, waiting for transfers between devices, exchange_sum(): paired = kept + lax.ppermute(away, axis, [(i, i ^ 1) for i in range(total)])  1.01 us
    broadcast_in_dim x1, other arithmetic, shards(): return (gradient[None], own[None, None])  0.63 us
    ppermute x1, starting transfers between devices, exchange_sum(): paired = kept + lax.ppermute(away, axis, [(i, i ^ 1) for i in range(total)])  0.56 us
  transfers between devices with their start and end apart: 4, of which 4 were waited for; matrix products, arithmetic and copies ran while one was open for 0% of the time, Pallas kernels for 0%

profile of v3, /device:TPU:0, one launch (start us, length us, event | category | flops | bytes accessed | tf_op | source)
XLA Modules:
  0.0 20.2 jit_solution(8608818805567425515)
XLA Ops:
  1.3 6.6 %local_terms.1 = (f32[4,72,128]{2,1,0:T(8,128)S(1)}, f32[4,72,128]{2,1,0:T(8,128)S(1)}, f32[64,256]{1,0:T(8,128)}) custom-call(s32[1]{0:T(128)S(6)} %copy.11.count_hbm, s32[1,256]{1,0:T(1,128)} %time_hbm.1, bf16[256,384]{1,0:T(8,128)(2,1)} %bitcast.24, bf16[384,768]{1,0:T(8,128)(2,1)} %constant.2.clone.fourier_hbm, bf16[128,384]{1,0:T(8,128)(2,1)} %bitcast.26, ...), custom_call_target="tpu_custom_call" | custom-call | tf_op jit(solution)/shard_map/local_terms/pallas_call | solution.py:288
  7.9 0.6 %collective-permute-start = (f32[4,72,128]{2,1,0:T(8,128)S(1)}, f32[4,72,128]{2,1,0:T(8,128)S(1)}, u32[]{:S(2)}, u32[]{:S(2)}) collective-permute-start(f32[4,72,128]{2,1,0:T(8,128)S(1)} %get-tuple-element.6), channel_id=1, source_target_pairs={{0,1},{1,0},{2,3},{3,2},{4,5},{5,4},{6,7},{7,6},{8,9},{9,8},{10,11... | collective-permute-start | bytes 442376 | tf_op jit(solution)/shard_map/ppermute | solution.py:320
  8.5 1.0 %collective-permute-done = f32[4,72,128]{2,1,0:T(8,128)S(1)} collective-permute-done((f32[4,72,128]{2,1,0:T(8,128)S(1)}, f32[4,72,128]{2,1,0:T(8,128)S(1)}, u32[]{:S(2)}, u32[]{:S(2)}) %collective-permute-start) | collective-permute-done | bytes 147488 | tf_op jit(solution)/shard_map/ppermute | solution.py:320
  9.5 3.0 %collective-permute-start.1 = (f32[72,128]{1,0:T(8,128)S(1)}, f32[72,128]{1,0:T(8,128)S(1)}, u32[]{:S(2)}, u32[]{:S(2)}) collective-permute-start(f32[72,128]{1,0:T(8,128)S(1)} %get-tuple-element.8), channel_id=1, source_target_pairs={{0,2},{1,3},{2,4},{3,5},{4,6},{5,7},{6,0},{7,1},{8,10},{9,11},{10,... | collective-permute-start | bytes 110600 | tf_op jit(solution)/shard_map/ppermute | solution.py:323
  12.5 2.1 %collective-permute-start.3 = (f32[72,128]{1,0:T(8,128)S(1)}, f32[72,128]{1,0:T(8,128)S(1)}, u32[]{:S(2)}, u32[]{:S(2)}) collective-permute-start(f32[72,128]{1,0:T(8,128)S(1)} %get-tuple-element.9), channel_id=1, source_target_pairs={{0,6},{1,7},{2,0},{3,1},{4,2},{5,3},{6,4},{7,5},{8,14},{9,15},{10,... | collective-permute-start | bytes 110600 | tf_op jit(solution)/shard_map/ppermute | solution.py:323
  14.6 0.9 %collective-permute-start.2 = (f32[72,128]{1,0:T(8,128)S(1)}, f32[72,128]{1,0:T(8,128)S(1)}, u32[]{:S(2)}, u32[]{:S(2)}) collective-permute-start(f32[72,128]{1,0:T(8,128)S(1)} %get-tuple-element.10), channel_id=1, source_target_pairs={{0,4},{1,5},{2,6},{3,7},{4,0},{5,1},{6,2},{7,3},{8,12},{9,13},{10,... | collective-permute-start | bytes 110600 | tf_op jit(solution)/shard_map/ppermute | solution.py:323
  15.5 1.0 %collective-permute-done.1 = f32[72,128]{1,0:T(8,128)S(1)} collective-permute-done((f32[72,128]{1,0:T(8,128)S(1)}, f32[72,128]{1,0:T(8,128)S(1)}, u32[]{:S(2)}, u32[]{:S(2)}) %collective-permute-start.1) | collective-permute-done | bytes 36896 | tf_op jit(solution)/shard_map/ppermute | solution.py:323
  16.6 0.3 %collective-permute-done.3 = f32[72,128]{1,0:T(8,128)S(1)} collective-permute-done((f32[72,128]{1,0:T(8,128)S(1)}, f32[72,128]{1,0:T(8,128)S(1)}, u32[]{:S(2)}, u32[]{:S(2)}) %collective-permute-start.3) | collective-permute-done | bytes 36896 | tf_op jit(solution)/shard_map/ppermute | solution.py:323
  16.9 2.6 %collective-permute-done.2 = f32[72,128]{1,0:T(8,128)S(1)} collective-permute-done((f32[72,128]{1,0:T(8,128)S(1)}, f32[72,128]{1,0:T(8,128)S(1)}, u32[]{:S(2)}, u32[]{:S(2)}) %collective-permute-start.2) | collective-permute-done | bytes 36896 | tf_op jit(solution)/shard_map/ppermute | solution.py:323
  19.5 0.1 fusion.3
  19.5 0.6 %maximum_bitcast_fusion = f32[1,48,192]{2,1,0:T(8,128)} fusion(f32[24,64]{1,0:T(8,128)S(1)} %get-tuple-element.12, f32[24,64]{1,0:T(8,128)S(1)} %get-tuple-element.11, f32[48,128]{1,0:T(8,128)S(1)} %slice.35), kind=kLoop, calls=%fused_computation | loop fusion | flops 18432 | bytes 73728 | tf_op jit(solution)/shard_map/broadcast_in_dim | solution.py:356
  (4 shorter events, 0.0 us)
Async XLA Ops:
  7.9 1.6 %collective-permute-start = (f32[4,72,128]{2,1,0:T(8,128)S(1)}, f32[4,72,128]{2,1,0:T(8,128)S(1)}, u32[]{:S(2)}, u32[]{:S(2)}) collective-permute-start(f32[4,72,128]{2,1,0:T(8,128)S(1)} %get-tuple-element.6), channel_id=1, source_target_pairs={{0,1},{1,0},{2,3},{3,2},{4,5},{5,4},{6,7},{7,6},{8,9},{9,8},{10,11... | collective-permute-start | bytes 442376 | tf_op jit(solution)/shard_map/ppermute | solution.py:320
  9.5 7.0 %collective-permute-start.1 = (f32[72,128]{1,0:T(8,128)S(1)}, f32[72,128]{1,0:T(8,128)S(1)}, u32[]{:S(2)}, u32[]{:S(2)}) collective-permute-start(f32[72,128]{1,0:T(8,128)S(1)} %get-tuple-element.8), channel_id=1, source_target_pairs={{0,2},{1,3},{2,4},{3,5},{4,6},{5,7},{6,0},{7,1},{8,10},{9,11},{10,... | collective-permute-start | bytes 110600 | tf_op jit(solution)/shard_map/ppermute | solution.py:323
  12.5 4.4 %collective-permute-start.3 = (f32[72,128]{1,0:T(8,128)S(1)}, f32[72,128]{1,0:T(8,128)S(1)}, u32[]{:S(2)}, u32[]{:S(2)}) collective-permute-start(f32[72,128]{1,0:T(8,128)S(1)} %get-tuple-element.9), channel_id=1, source_target_pairs={{0,6},{1,7},{2,0},{3,1},{4,2},{5,3},{6,4},{7,5},{8,14},{9,15},{10,... | collective-permute-start | bytes 110600 | tf_op jit(solution)/shard_map/ppermute | solution.py:323
  14.6 4.9 %collective-permute-start.2 = (f32[72,128]{1,0:T(8,128)S(1)}, f32[72,128]{1,0:T(8,128)S(1)}, u32[]{:S(2)}, u32[]{:S(2)}) collective-permute-start(f32[72,128]{1,0:T(8,128)S(1)} %get-tuple-element.10), channel_id=1, source_target_pairs={{0,4},{1,5},{2,6},{3,7},{4,0},{5,1},{6,2},{7,3},{8,12},{9,13},{10,... | collective-permute-start | bytes 110600 | tf_op jit(solution)/shard_map/ppermute | solution.py:323

commit v4 on v3

--- a/solution.py
+++ b/solution.py
@@ -12,9 +12,9 @@
 SUBSTEPS = 4
 LANES = 128
 WINDOW = 256
-CHUNK = 128
+CHUNK = 192
+HALF = 192
 PIECE = 16
-TALL = 48
 
 
 def dft_tables(length):
@@ -28,16 +28,33 @@
     return lax.dot_general(a, b, (contract, ((), ())), preferred_element_type=jnp.float32)
 
 
-def sine_cosine(x):
-    y = x * x
-    sine = -1.0 / math.factorial(11)
-    for power in (9, 7, 5, 3):
-        sine = sine * y + (-1.0) ** (power // 2) / math.factorial(power)
-    sine = x * (sine * y + 1.0)
-    cosine = 1.0 / math.factorial(12)
-    for power in (10, 8, 6, 4, 2):
-        cosine = cosine * y + (-1.0) ** (power // 2) / math.factorial(power)
-    return sine, cosine * y + 1.0
+SINE = (
+    0.49999999863922073,
+    -0.020833325771248395,
+    0.00026040993453922765,
+    -1.5479976876565651e-06,
+    5.113416832465264e-09,
+)
+COSINE = (
+    0.999999999872559,
+    -0.12499999898030063,
+    0.002604165343651872,
+    -2.170076051907257e-05,
+    9.674607230271745e-08,
+    -2.5566742521071554e-10,
+)
+
+
+def polynomial(terms, z):
+    total = terms[-1] * z + terms[-2]
+    for term in terms[-3::-1]:
+        total = total * z + term
+    return total
+
+
+def half_angle(field):
+    z = field * field
+    return field * polynomial(SINE, z), polynomial(COSINE, z)
 
 
 def pack(block):
@@ -98,7 +115,7 @@
     right_ref,
     inner_ref,
     misfit_ref,
-    adjoint_ref,
+    row_ref,
     turned_ref,
     scaled_ref,
     back_ref,
@@ -134,30 +151,45 @@
     ]
     for copy in copies:
         copy.start()
-    for copy in copies[:4]:
+    for copy in copies[:5]:
         copy.wait()
 
-    grid_rows = rows_ref[...]
-    grid_cols = cols_ref[...]
     fourier = fourier_ref[...]
-    row_op = dot(grid_rows, fourier).astype(jnp.bfloat16)
-    for part in range(2):
-        span = slice(part * pixels, (part + 1) * pixels)
-        adjoint_ref[:, part * row_total : (part + 1) * row_total] = dot(
-            fourier[:, span], grid_rows, ((1,), (1,))
-        ).astype(jnp.bfloat16)
-    col_op = dot(grid_cols, fourier).astype(jnp.bfloat16)
+    row_op = dot(rows_ref[...], fourier).astype(jnp.bfloat16)
+    row_ref[...] = row_op
+    col_op = dot(cols_ref[...], fourier).astype(jnp.bfloat16)
     left_ref[:col_total, :pixels] = col_op[:, :pixels]
     left_ref[:col_total, pixels:] = -col_op[:, pixels:]
     left_ref[col_total:, :pixels] = col_op[:, pixels:]
     left_ref[col_total:, pixels:] = col_op[:, :pixels]
-    col_re = dot(fourier[:, :pixels], grid_cols, ((1,), (1,))).astype(jnp.bfloat16)
-    col_im = dot(fourier[:, pixels:], grid_cols, ((1,), (1,))).astype(jnp.bfloat16)
+    col_re = jnp.transpose(col_op[:, :pixels])
+    col_im = jnp.transpose(col_op[:, pixels:])
     right_ref[:pixels, :col_total] = col_re
     right_ref[:pixels, col_total:] = col_im
     right_ref[pixels:, :col_total] = -col_im
     right_ref[pixels:, col_total:] = col_re
 
+    for low in range(0, pixels, PIECE):
+        rows = slice(low, low + PIECE)
+        sine, cosine = half_angle(field_ref[rows, :])
+        twice = 4.0 * (cosine * cosine) - 2.0
+        previous = (cosine, -sine)
+        for pair in range(pairs):
+            if pair == 1:
+                previous, cosine, sine = (
+                    (cosine, sine),
+                    twice * cosine - cosine,
+                    twice * sine + sine,
+                )
+            elif pair:
+                previous, cosine, sine = (
+                    (cosine, sine),
+                    twice * cosine - previous[0],
+                    twice * sine - previous[1],
+                )
+            phase_ref[2 * pair, rows, :] = cosine
+            phase_ref[2 * pair + 1, rows, :] = sine
+
     steps = jnp.broadcast_to(time_ref[...].astype(jnp.float32), (8, row_total))
 
     def weight(s):
@@ -167,40 +199,35 @@
     for pair in range(pairs):
         above, below = weight(pairs + pair), weight(pairs - 1 - pair)
         along += [above + below, above - below]
-    adjoint = adjoint_ref[...]
-    for i in range(seg_total):
-        scale = jnp.concatenate([along[i][:1]] * 2, 1).astype(jnp.bfloat16)
-        scaled_ref[i] = adjoint * scale
-
-    for copy in copies[4:7]:
+    for part in range(2):
+        adjoint = jnp.transpose(row_op[:, part * pixels : (part + 1) * pixels])
+        columns = slice(part * row_total, (part + 1) * row_total)
+        for i in range(seg_total):
+            scaled = adjoint * along[i][:1].astype(jnp.bfloat16)
+            for half in range(pixels // HALF):
+                scaled_ref[half, i * HALF : (i + 1) * HALF, columns] = scaled[
+                    half * HALF : (half + 1) * HALF
+                ]
+
+    for copy in copies[5:7]:
         copy.wait()
     right = right_ref[...]
     for chunk in range(pixels // CHUNK):
         for low in range(0, CHUNK, PIECE):
             rows = slice(chunk * CHUNK + low, chunk * CHUNK + low + PIECE)
-            sine, cosine = sine_cosine(0.5 * field_ref[rows, :])
-            image_re = image_ref[rows, :pixels].astype(jnp.float32)
-            image_im = image_ref[rows, pixels:].astype(jnp.float32)
-            map_re = maps_ref[rows, :pixels].astype(jnp.float32)
-            map_im = maps_ref[rows, pixels:].astype(jnp.float32)
+            image_re, image_im = image_ref[rows, :pixels], image_ref[rows, pixels:]
+            map_re, map_im = maps_ref[rows, :pixels], maps_ref[rows, pixels:]
             base_re = image_re * map_re - image_im * map_im
             base_im = image_re * map_im + image_im * map_re
-            twice_re = cosine * cosine - sine * sine
-            twice_im = 2.0 * cosine * sine
             for pair in range(pairs):
-                if pair:
-                    cosine, sine = (
-                        cosine * twice_re - sine * twice_im,
-                        cosine * twice_im + sine * twice_re,
-                    )
-                phase_ref[2 * pair, rows, :] = cosine
-                phase_ref[2 * pair + 1, rows, :] = sine
+                cosine = phase_ref[2 * pair, rows, :].astype(jnp.bfloat16)
+                sine = phase_ref[2 * pair + 1, rows, :].astype(jnp.bfloat16)
                 even = slice(2 * pair * CHUNK + low, 2 * pair * CHUNK + low + PIECE)
                 odd = slice(even.start + CHUNK, even.stop + CHUNK)
-                wave_ref[chunk, even, :pixels] = (base_re * cosine).astype(jnp.bfloat16)
-                wave_ref[chunk, even, pixels:] = (base_im * cosine).astype(jnp.bfloat16)
-                wave_ref[chunk, odd, :pixels] = (-base_im * sine).astype(jnp.bfloat16)
-                wave_ref[chunk, odd, pixels:] = (base_re * sine).astype(jnp.bfloat16)
+                wave_ref[chunk, even, :pixels] = base_re * cosine
+                wave_ref[chunk, even, pixels:] = base_im * cosine
+                wave_ref[chunk, odd, :pixels] = -base_im * sine
+                wave_ref[chunk, odd, pixels:] = base_re * sine
         v = dot(wave_ref[chunk], right).astype(jnp.bfloat16)
         for i in range(seg_total):
             piece = v[i * CHUNK : (i + 1) * CHUNK]
@@ -211,14 +238,14 @@
             inner_ref[i, second, col_total:] = piece[:, :col_total]
     samples = None
     for i in range(seg_total):
-        y = dot(row_op, inner_ref[i]) * jnp.transpose(along[i])[:, :1]
+        y = dot(row_ref[...], inner_ref[i]) * jnp.transpose(along[i])[:, :1]
         samples = y if samples is None else samples + y
 
     copies[7].wait()
     copies[8].wait()
     row_ids = lax.broadcasted_iota(jnp.int32, (row_total, 2 * col_total), 0)
     misfit = samples - measured_ref[...].astype(jnp.float32)
-    misfit = jnp.where(row_ids < count_ref[0], misfit, 0.0)
+    misfit = jnp.where(row_ids < count_ref[...], misfit, 0.0)
     misfit_ref[...] = misfit
     own_start = pl.multiple_of(segment * own_rows, own_rows)
     own_copy = pltpu.make_async_copy(misfit_ref.at[pl.ds(own_start, own_rows)], own_ref, sems.at[9])
@@ -239,25 +266,27 @@
     turned_ref[row_total:, WINDOW:] = -turn_re
     turned = turned_ref[...]
     factor = coil_total ** (-0.5)
-    for i in range(seg_total):
-        back_ref[i] = dot(scaled_ref[i], turned)
-    for low in range(0, pixels, TALL):
-        rows = slice(low, low + TALL)
-        sum_re = None
-        for pair in range(pairs):
-            cosine = phase_ref[2 * pair, rows, pl.ds(start, WINDOW)]
-            sine = phase_ref[2 * pair + 1, rows, pl.ds(start, WINDOW)]
-            add_re = cosine * back_ref[2 * pair, rows, :WINDOW]
-            add_re = add_re + sine * back_ref[2 * pair + 1, rows, WINDOW:]
-            add_im = cosine * back_ref[2 * pair, rows, WINDOW:]
-            add_im = add_im - sine * back_ref[2 * pair + 1, rows, :WINDOW]
-            sum_re = add_re if sum_re is None else sum_re + add_re
-            sum_im = add_im if pair == 0 else sum_im + add_im
-        map_re = maps_ref[rows, pl.ds(start, WINDOW)].astype(jnp.float32)
-        map_im = maps_ref[rows, pl.ds(after, WINDOW)].astype(jnp.float32)
-        first = jnp.where(imaginary, -map_im, map_re) * factor
-        second = jnp.where(imaginary, map_re, map_im) * factor
-        term_ref[rows, :] = pltpu.roll(first * sum_re + second * sum_im, shift, 1)
+    for half in range(pixels // HALF):
+        back_ref[half] = dot(scaled_ref[half], turned)
+        for low in range(0, HALF, PIECE):
+            rows = slice(half * HALF + low, half * HALF + low + PIECE)
+            sum_re = None
+            for pair in range(pairs):
+                cosine = phase_ref[2 * pair, rows, pl.ds(start, WINDOW)]
+                sine = phase_ref[2 * pair + 1, rows, pl.ds(start, WINDOW)]
+                even = slice(2 * pair * HALF + low, 2 * pair * HALF + low + PIECE)
+                odd = slice(even.start + HALF, even.stop + HALF)
+                add_re = cosine * back_ref[half, even, :WINDOW]
+                add_re = add_re + sine * back_ref[half, odd, WINDOW:]
+                add_im = cosine * back_ref[half, even, WINDOW:]
+                add_im = add_im - sine * back_ref[half, odd, :WINDOW]
+                sum_re = add_re if sum_re is None else sum_re + add_re
+                sum_im = add_im if pair == 0 else sum_im + add_im
+            map_re = maps_ref[rows, pl.ds(start, WINDOW)].astype(jnp.float32)
+            map_im = maps_ref[rows, pl.ds(after, WINDOW)].astype(jnp.float32)
+            first = jnp.where(imaginary, -map_im, map_re) * factor
+            second = jnp.where(imaginary, map_re, map_im) * factor
+            term_ref[rows, :] = pltpu.roll(first * sum_re + second * sum_im, shift, 1)
 
     lane = lax.rem(member, 2)
     group = member // 2
@@ -294,8 +323,7 @@
         ),
         in_specs=[anywhere] * (1 + len(operands)),
         out_specs=(vmem, vmem, anywhere),
-        scratch_shapes=[pltpu.SMEM(count.shape, count.dtype)]
-        + [pltpu.VMEM(x.shape, x.dtype) for x in operands]
+        scratch_shapes=[pltpu.VMEM(x.shape, x.dtype) for x in (count, *operands)]
         + [
             pltpu.VMEM((pixels // CHUNK, seg_total * CHUNK, 2 * pixels), jnp.bfloat16),
             pltpu.VMEM((seg_total, pixels, pixels), jnp.float32),
@@ -303,10 +331,10 @@
             pltpu.VMEM((2 * pixels, 2 * col_total), jnp.bfloat16),
             pltpu.VMEM((seg_total, 2 * pixels, 2 * col_total), jnp.bfloat16),
             pltpu.VMEM((row_total, 2 * col_total), jnp.float32),
-            pltpu.VMEM((pixels, 2 * row_total), jnp.bfloat16),
+            pltpu.VMEM((row_total, 2 * pixels), jnp.bfloat16),
             pltpu.VMEM((2 * row_total, 2 * WINDOW), jnp.bfloat16),
-            pltpu.VMEM((seg_total, pixels, 2 * row_total), jnp.bfloat16),
-            pltpu.VMEM((seg_total, pixels, 2 * WINDOW), jnp.float32),
+            pltpu.VMEM((pixels // HALF, seg_total * HALF, 2 * row_total), jnp.bfloat16),
+            pltpu.VMEM((pixels // HALF, seg_total * HALF, 2 * WINDOW), jnp.float32),
             pltpu.VMEM((pixels, WINDOW), jnp.float32),
             pltpu.SemaphoreType.DMA((10,)),
         ],
@@ -349,7 +377,7 @@
         interp_cols[0],
         measured[0, 0],
         sample_time,
-        sample_count,
+        sample_count.reshape(1, 1),
     )
     total = exchange_sum(kept, away, "coil")
     gradient = unpack(total, pixels // coil_total, 2 * pixels // seg_total)

time: 20.3 us -> 19.6 us (0.966)
  Pallas kernels: 6.63 us -> 5.87 us
    pallas_call x1, Pallas kernels: 6.63 us -> 5.87 us  [local_terms(): pl.pallas_call(functools.partial(local_kernel, seg_total, coil_total), ou...]
where the time goes in v4:
time: 19.6 us; the launch traced here: 19.4 us
  starting transfers between devices  6.57 us (34%)
  Pallas kernels  5.87 us (30%)
  waiting for transfers between devices  4.91 us (25%)
  between operations  1.31 us (7%)
  other arithmetic  0.66 us (3%)
    ppermute x3, starting transfers between devices, exchange_sum(): lax.ppermute(paired[step], axis, [(i, (i + 2 * step) % total) for i in ra...  6.01 us
    pallas_call x1, Pallas kernels, local_terms(): pl.pallas_call(functools.partial(local_kernel, seg_total, coil_total), ou...  5.87 us
    ppermute x3, waiting for transfers between devices, exchange_sum(): lax.ppermute(paired[step], axis, [(i, (i + 2 * step) % total) for i in ra...  3.91 us
    ppermute x1, waiting for transfers between devices, exchange_sum(): paired = kept + lax.ppermute(away, axis, [(i, i ^ 1) for i in range(total)])  1.01 us
    broadcast_in_dim x1, other arithmetic, shards(): return (gradient[None], own[None, None])  0.63 us
    ppermute x1, starting transfers between devices, exchange_sum(): paired = kept + lax.ppermute(away, axis, [(i, i ^ 1) for i in range(total)])  0.56 us
  transfers between devices with their start and end apart: 4, of which 4 were waited for; matrix products, arithmetic and copies ran while one was open for 0% of the time, Pallas kernels for 0%

profile of v4, /device:TPU:0, one launch (start us, length us, event | category | flops | bytes accessed | tf_op | source)
XLA Modules:
  0.0 19.4 jit_solution(10898555361172772444)
XLA Ops:
  1.3 5.9 %local_terms.1 = (f32[4,72,128]{2,1,0:T(8,128)S(1)}, f32[4,72,128]{2,1,0:T(8,128)S(1)}, f32[64,256]{1,0:T(8,128)}) custom-call(s32[1,1]{1,0:T(1,128)} %bitcast.23.count_hbm, s32[1,256]{1,0:T(1,128)} %time_hbm.1, bf16[256,384]{1,0:T(8,128)(2,1)} %bitcast.26, bf16[384,768]{1,0:T(8,128)(2,1)} %constant.2.clone.fourier_hbm, bf16[128,384]{1,0:T(8,128)(2,1)} %bitcast.28, ...), custom_call_target="tpu_custom_call" | custom-call | tf_op jit(solution)/shard_map/local_terms/pallas_call | solution.py:317
  7.2 0.6 %collective-permute-start = (f32[4,72,128]{2,1,0:T(8,128)S(1)}, f32[4,72,128]{2,1,0:T(8,128)S(1)}, u32[]{:S(2)}, u32[]{:S(2)}) collective-permute-start(f32[4,72,128]{2,1,0:T(8,128)S(1)} %get-tuple-element.6), channel_id=1, source_target_pairs={{0,1},{1,0},{2,3},{3,2},{4,5},{5,4},{6,7},{7,6},{8,9},{9,8},{10,11... | collective-permute-start | bytes 442376 | tf_op jit(solution)/shard_map/ppermute | solution.py:348
  7.7 1.0 %collective-permute-done = f32[4,72,128]{2,1,0:T(8,128)S(1)} collective-permute-done((f32[4,72,128]{2,1,0:T(8,128)S(1)}, f32[4,72,128]{2,1,0:T(8,128)S(1)}, u32[]{:S(2)}, u32[]{:S(2)}) %collective-permute-start) | collective-permute-done | bytes 147488 | tf_op jit(solution)/shard_map/ppermute | solution.py:348
  8.8 3.0 %collective-permute-start.1 = (f32[72,128]{1,0:T(8,128)S(1)}, f32[72,128]{1,0:T(8,128)S(1)}, u32[]{:S(2)}, u32[]{:S(2)}) collective-permute-start(f32[72,128]{1,0:T(8,128)S(1)} %get-tuple-element.8), channel_id=1, source_target_pairs={{0,2},{1,3},{2,4},{3,5},{4,6},{5,7},{6,0},{7,1},{8,10},{9,11},{10,... | collective-permute-start | bytes 110600 | tf_op jit(solution)/shard_map/ppermute | solution.py:351
  11.7 2.1 %collective-permute-start.3 = (f32[72,128]{1,0:T(8,128)S(1)}, f32[72,128]{1,0:T(8,128)S(1)}, u32[]{:S(2)}, u32[]{:S(2)}) collective-permute-start(f32[72,128]{1,0:T(8,128)S(1)} %get-tuple-element.9), channel_id=1, source_target_pairs={{0,6},{1,7},{2,0},{3,1},{4,2},{5,3},{6,4},{7,5},{8,14},{9,15},{10,... | collective-permute-start | bytes 110600 | tf_op jit(solution)/shard_map/ppermute | solution.py:351
  13.8 0.9 %collective-permute-start.2 = (f32[72,128]{1,0:T(8,128)S(1)}, f32[72,128]{1,0:T(8,128)S(1)}, u32[]{:S(2)}, u32[]{:S(2)}) collective-permute-start(f32[72,128]{1,0:T(8,128)S(1)} %get-tuple-element.10), channel_id=1, source_target_pairs={{0,4},{1,5},{2,6},{3,7},{4,0},{5,1},{6,2},{7,3},{8,12},{9,13},{10,... | collective-permute-start | bytes 110600 | tf_op jit(solution)/shard_map/ppermute | solution.py:351
  14.8 1.0 %collective-permute-done.1 = f32[72,128]{1,0:T(8,128)S(1)} collective-permute-done((f32[72,128]{1,0:T(8,128)S(1)}, f32[72,128]{1,0:T(8,128)S(1)}, u32[]{:S(2)}, u32[]{:S(2)}) %collective-permute-start.1) | collective-permute-done | bytes 36896 | tf_op jit(solution)/shard_map/ppermute | solution.py:351
  15.8 0.3 %collective-permute-done.3 = f32[72,128]{1,0:T(8,128)S(1)} collective-permute-done((f32[72,128]{1,0:T(8,128)S(1)}, f32[72,128]{1,0:T(8,128)S(1)}, u32[]{:S(2)}, u32[]{:S(2)}) %collective-permute-start.3) | collective-permute-done | bytes 36896 | tf_op jit(solution)/shard_map/ppermute | solution.py:351
  16.1 2.6 %collective-permute-done.2 = f32[72,128]{1,0:T(8,128)S(1)} collective-permute-done((f32[72,128]{1,0:T(8,128)S(1)}, f32[72,128]{1,0:T(8,128)S(1)}, u32[]{:S(2)}, u32[]{:S(2)}) %collective-permute-start.2) | collective-permute-done | bytes 36896 | tf_op jit(solution)/shard_map/ppermute | solution.py:351
  18.7 0.1 fusion.3
  18.8 0.6 %maximum_bitcast_fusion = f32[1,48,192]{2,1,0:T(8,128)} fusion(f32[24,64]{1,0:T(8,128)S(1)} %get-tuple-element.12, f32[24,64]{1,0:T(8,128)S(1)} %get-tuple-element.11, f32[48,128]{1,0:T(8,128)S(1)} %slice.35), kind=kLoop, calls=%fused_computation | loop fusion | flops 18432 | bytes 73728 | tf_op jit(solution)/shard_map/broadcast_in_dim | solution.py:384
  (4 shorter events, 0.0 us)
Async XLA Ops:
  7.2 1.6 %collective-permute-start = (f32[4,72,128]{2,1,0:T(8,128)S(1)}, f32[4,72,128]{2,1,0:T(8,128)S(1)}, u32[]{:S(2)}, u32[]{:S(2)}) collective-permute-start(f32[4,72,128]{2,1,0:T(8,128)S(1)} %get-tuple-element.6), channel_id=1, source_target_pairs={{0,1},{1,0},{2,3},{3,2},{4,5},{5,4},{6,7},{7,6},{8,9},{9,8},{10,11... | collective-permute-start | bytes 442376 | tf_op jit(solution)/shard_map/ppermute | solution.py:348
  8.8 7.0 %collective-permute-start.1 = (f32[72,128]{1,0:T(8,128)S(1)}, f32[72,128]{1,0:T(8,128)S(1)}, u32[]{:S(2)}, u32[]{:S(2)}) collective-permute-start(f32[72,128]{1,0:T(8,128)S(1)} %get-tuple-element.8), channel_id=1, source_target_pairs={{0,2},{1,3},{2,4},{3,5},{4,6},{5,7},{6,0},{7,1},{8,10},{9,11},{10,... | collective-permute-start | bytes 110600 | tf_op jit(solution)/shard_map/ppermute | solution.py:351
  11.7 4.4 %collective-permute-start.3 = (f32[72,128]{1,0:T(8,128)S(1)}, f32[72,128]{1,0:T(8,128)S(1)}, u32[]{:S(2)}, u32[]{:S(2)}) collective-permute-start(f32[72,128]{1,0:T(8,128)S(1)} %get-tuple-element.9), channel_id=1, source_target_pairs={{0,6},{1,7},{2,0},{3,1},{4,2},{5,3},{6,4},{7,5},{8,14},{9,15},{10,... | collective-permute-start | bytes 110600 | tf_op jit(solution)/shard_map/ppermute | solution.py:351
  13.8 4.9 %collective-permute-start.2 = (f32[72,128]{1,0:T(8,128)S(1)}, f32[72,128]{1,0:T(8,128)S(1)}, u32[]{:S(2)}, u32[]{:S(2)}) collective-permute-start(f32[72,128]{1,0:T(8,128)S(1)} %get-tuple-element.10), channel_id=1, source_target_pairs={{0,4},{1,5},{2,6},{3,7},{4,0},{5,1},{6,2},{7,3},{8,12},{9,13},{10,... | collective-permute-start | bytes 110600 | tf_op jit(solution)/shard_map/ppermute | solution.py:351

commit v5 on v4

--- a/solution.py
+++ b/solution.py
@@ -291,7 +291,7 @@
     lane = lax.rem(member, 2)
     group = member // 2
     for g in range(groups):
-        slot = lax.rem(g + groups - group, groups)
+        slot = slot_of(g, group, groups)
         upper = term_ref[2 * g * block_rows : (2 * g + 1) * block_rows, :width]
         lower = term_ref[(2 * g + 1) * block_rows : (2 * g + 2) * block_rows, :width]
         for ref, value in (
@@ -343,14 +343,29 @@
     )(count, *operands)
 
 
+def routes(groups):
+    if groups == 4:
+        return [(2, 3, 1, 0), (3, 2, 0, 1), (1, 0, 3, 2)]
+    return [tuple((z + step) % groups for z in range(groups)) for step in range(1, groups)]
+
+
+def slot_of(target, group, groups):
+    if groups != 4:
+        return lax.rem(target + groups - group, groups)
+    slot = jnp.int32(0)
+    for k, route in enumerate(routes(groups)):
+        slot = jnp.where(group == route.index(target), k + 1, slot)
+    return slot
+
+
 def exchange_sum(kept, away, axis):
     total = lax.axis_size(axis)
     paired = kept + lax.ppermute(away, axis, [(i, i ^ 1) for i in range(total)])
     result = paired[0]
-    for step in range(1, total // 2):
-        result = result + lax.ppermute(
-            paired[step], axis, [(i, (i + 2 * step) % total) for i in range(total)]
-        )
+    for k, route in enumerate(routes(total // 2)):
+        pairs = [(i, 2 * route[i // 2] + i % 2) for i in range(total)]
+        got = lax.ppermute(paired[k + 1], axis, pairs)
+        result = result + got
     return result
 
 
@@ -387,4 +402,6 @@
 def solution(mesh):
     in_specs = (P(), P("coil", None, None), P(), P(), P(), P("coil", None, None, None), P(), P())
     out_specs = (P(None, "coil", "seg"), P("coil", None, "seg", None))
-    return jax.shard_map(shards, mesh=mesh, in_specs=in_specs, out_specs=out_specs, check_vma=False)
+    return jax.shard_map(
+        shards, mesh=mesh, in_specs=in_specs, out_specs=out_specs, check_vma=False
+    )

time: 19.6 us -> 20.2 us (1.031)
  waiting for transfers between devices: 4.91 us -> 5.81 us
    ppermute x3, waiting for transfers between devices: 3.91 us -> 4.8 us  [exchange_sum(): got = lax.ppermute(paired[k + 1], axis, pairs)]
where the time goes in v5:
time: 20.2 us; the launch traced here: 20.1 us
  starting transfers between devices  6.46 us (32%)
  waiting for transfers between devices  5.81 us (29%)
  Pallas kernels  5.75 us (28%)
  between operations  1.31 us (6%)
  other arithmetic  0.66 us (3%)
    ppermute x3, starting transfers between devices, exchange_sum(): got = lax.ppermute(paired[k + 1], axis, pairs)  5.9 us
    pallas_call x1, Pallas kernels, local_terms(): pl.pallas_call(functools.partial(local_kernel, seg_total, coil_total), ou...  5.75 us
    ppermute x3, waiting for transfers between devices, exchange_sum(): got = lax.ppermute(paired[k + 1], axis, pairs)  4.8 us
    ppermute x1, waiting for transfers between devices, exchange_sum(): paired = kept + lax.ppermute(away, axis, [(i, i ^ 1) for i in range(total)])  1.01 us
    broadcast_in_dim x1, other arithmetic, shards(): return (gradient[None], own[None, None])  0.63 us
    ppermute x1, starting transfers between devices, exchange_sum(): paired = kept + lax.ppermute(away, axis, [(i, i ^ 1) for i in range(total)])  0.56 us
  transfers between devices with their start and end apart: 4, of which 4 were waited for; matrix products, arithmetic and copies ran while one was open for 0% of the time, Pallas kernels for 0%

profile of v5, /device:TPU:0, one launch (start us, length us, event | category | flops | bytes accessed | tf_op | source)
XLA Modules:
  0.0 20.1 jit_solution(14600308362229526817)
XLA Ops:
  1.3 5.8 %local_terms.1 = (f32[4,72,128]{2,1,0:T(8,128)S(1)}, f32[4,72,128]{2,1,0:T(8,128)S(1)}, f32[64,256]{1,0:T(8,128)}) custom-call(s32[1,1]{1,0:T(1,128)} %bitcast.23.count_hbm, s32[1,256]{1,0:T(1,128)} %time_hbm.1, bf16[256,384]{1,0:T(8,128)(2,1)} %bitcast.26, bf16[384,768]{1,0:T(8,128)(2,1)} %constant.2.clone.fourier_hbm, bf16[128,384]{1,0:T(8,128)(2,1)} %bitcast.28, ...), custom_call_target="tpu_custom_call" | custom-call | tf_op jit(solution)/shard_map/local_terms/pallas_call | solution.py:317
  7.0 0.6 %collective-permute-start = (f32[4,72,128]{2,1,0:T(8,128)S(1)}, f32[4,72,128]{2,1,0:T(8,128)S(1)}, u32[]{:S(2)}, u32[]{:S(2)}) collective-permute-start(f32[4,72,128]{2,1,0:T(8,128)S(1)} %get-tuple-element.6), channel_id=1, source_target_pairs={{0,1},{1,0},{2,3},{3,2},{4,5},{5,4},{6,7},{7,6},{8,9},{9,8},{10,11... | collective-permute-start | bytes 442376 | tf_op jit(solution)/shard_map/ppermute | solution.py:363
  7.6 1.0 %collective-permute-done = f32[4,72,128]{2,1,0:T(8,128)S(1)} collective-permute-done((f32[4,72,128]{2,1,0:T(8,128)S(1)}, f32[4,72,128]{2,1,0:T(8,128)S(1)}, u32[]{:S(2)}, u32[]{:S(2)}) %collective-permute-start) | collective-permute-done | bytes 147488 | tf_op jit(solution)/shard_map/ppermute | solution.py:363
  8.6 4.0 %collective-permute-start.1 = (f32[72,128]{1,0:T(8,128)S(1)}, f32[72,128]{1,0:T(8,128)S(1)}, u32[]{:S(2)}, u32[]{:S(2)}) collective-permute-start(f32[72,128]{1,0:T(8,128)S(1)} %get-tuple-element.8), channel_id=1, source_target_pairs={{0,4},{1,5},{2,6},{3,7},{4,2},{5,3},{6,0},{7,1},{8,12},{9,13},{10,... | collective-permute-start | bytes 110600 | tf_op jit(solution)/shard_map/ppermute | solution.py:367
  12.6 1.6 %collective-permute-start.3 = (f32[72,128]{1,0:T(8,128)S(1)}, f32[72,128]{1,0:T(8,128)S(1)}, u32[]{:S(2)}, u32[]{:S(2)}) collective-permute-start(f32[72,128]{1,0:T(8,128)S(1)} %get-tuple-element.9), channel_id=1, source_target_pairs={{0,2},{1,3},{2,0},{3,1},{4,6},{5,7},{6,4},{7,5},{8,10},{9,11},{10,... | collective-permute-start | bytes 110600 | tf_op jit(solution)/shard_map/ppermute | solution.py:367
  14.2 0.3 %collective-permute-start.2 = (f32[72,128]{1,0:T(8,128)S(1)}, f32[72,128]{1,0:T(8,128)S(1)}, u32[]{:S(2)}, u32[]{:S(2)}) collective-permute-start(f32[72,128]{1,0:T(8,128)S(1)} %get-tuple-element.10), channel_id=1, source_target_pairs={{0,6},{1,7},{2,4},{3,5},{4,0},{5,1},{6,2},{7,3},{8,14},{9,15},{10,... | collective-permute-start | bytes 110600 | tf_op jit(solution)/shard_map/ppermute | solution.py:367
  14.5 1.3 %collective-permute-done.1 = f32[72,128]{1,0:T(8,128)S(1)} collective-permute-done((f32[72,128]{1,0:T(8,128)S(1)}, f32[72,128]{1,0:T(8,128)S(1)}, u32[]{:S(2)}, u32[]{:S(2)}) %collective-permute-start.1) | collective-permute-done | bytes 36896 | tf_op jit(solution)/shard_map/ppermute | solution.py:367
  15.8 0.8 %collective-permute-done.3 = f32[72,128]{1,0:T(8,128)S(1)} collective-permute-done((f32[72,128]{1,0:T(8,128)S(1)}, f32[72,128]{1,0:T(8,128)S(1)}, u32[]{:S(2)}, u32[]{:S(2)}) %collective-permute-start.3) | collective-permute-done | bytes 36896 | tf_op jit(solution)/shard_map/ppermute | solution.py:367
  16.6 2.8 %collective-permute-done.2 = f32[72,128]{1,0:T(8,128)S(1)} collective-permute-done((f32[72,128]{1,0:T(8,128)S(1)}, f32[72,128]{1,0:T(8,128)S(1)}, u32[]{:S(2)}, u32[]{:S(2)}) %collective-permute-start.2) | collective-permute-done | bytes 36896 | tf_op jit(solution)/shard_map/ppermute | solution.py:367
  19.4 0.1 fusion.3
  19.4 0.6 %maximum_bitcast_fusion = f32[1,48,192]{2,1,0:T(8,128)} fusion(f32[24,64]{1,0:T(8,128)S(1)} %get-tuple-element.12, f32[24,64]{1,0:T(8,128)S(1)} %get-tuple-element.11, f32[48,128]{1,0:T(8,128)S(1)} %slice.35), kind=kLoop, calls=%fused_computation | loop fusion | flops 18432 | bytes 73728 | tf_op jit(solution)/shard_map/broadcast_in_dim | solution.py:399
  (4 shorter events, 0.0 us)
Async XLA Ops:
  7.0 1.6 %collective-permute-start = (f32[4,72,128]{2,1,0:T(8,128)S(1)}, f32[4,72,128]{2,1,0:T(8,128)S(1)}, u32[]{:S(2)}, u32[]{:S(2)}) collective-permute-start(f32[4,72,128]{2,1,0:T(8,128)S(1)} %get-tuple-element.6), channel_id=1, source_target_pairs={{0,1},{1,0},{2,3},{3,2},{4,5},{5,4},{6,7},{7,6},{8,9},{9,8},{10,11... | collective-permute-start | bytes 442376 | tf_op jit(solution)/shard_map/ppermute | solution.py:363
  8.6 7.2 %collective-permute-start.1 = (f32[72,128]{1,0:T(8,128)S(1)}, f32[72,128]{1,0:T(8,128)S(1)}, u32[]{:S(2)}, u32[]{:S(2)}) collective-permute-start(f32[72,128]{1,0:T(8,128)S(1)} %get-tuple-element.8), channel_id=1, source_target_pairs={{0,4},{1,5},{2,6},{3,7},{4,2},{5,3},{6,0},{7,1},{8,12},{9,13},{10,... | collective-permute-start | bytes 110600 | tf_op jit(solution)/shard_map/ppermute | solution.py:367
  12.6 4.0 %collective-permute-start.3 = (f32[72,128]{1,0:T(8,128)S(1)}, f32[72,128]{1,0:T(8,128)S(1)}, u32[]{:S(2)}, u32[]{:S(2)}) collective-permute-start(f32[72,128]{1,0:T(8,128)S(1)} %get-tuple-element.9), channel_id=1, source_target_pairs={{0,2},{1,3},{2,0},{3,1},{4,6},{5,7},{6,4},{7,5},{8,10},{9,11},{10,... | collective-permute-start | bytes 110600 | tf_op jit(solution)/shard_map/ppermute | solution.py:367
  14.2 5.1 %collective-permute-start.2 = (f32[72,128]{1,0:T(8,128)S(1)}, f32[72,128]{1,0:T(8,128)S(1)}, u32[]{:S(2)}, u32[]{:S(2)}) collective-permute-start(f32[72,128]{1,0:T(8,128)S(1)} %get-tuple-element.10), channel_id=1, source_target_pairs={{0,6},{1,7},{2,4},{3,5},{4,0},{5,1},{6,2},{7,3},{8,14},{9,15},{10,... | collective-permute-start | bytes 110600 | tf_op jit(solution)/shard_map/ppermute | solution.py:367

commit v6 on v5

--- a/solution.py
+++ b/solution.py
@@ -13,7 +13,8 @@
 LANES = 128
 WINDOW = 256
 CHUNK = 192
-HALF = 192
+EARLY = 256
+CUTS = (192, 384)
 PIECE = 16
 
 
@@ -88,7 +89,7 @@
 def local_kernel(
     seg_total,
     coil_total,
-    count_hbm,
+    count_ref,
     time_hbm,
     rows_hbm,
     fourier_hbm,
@@ -100,7 +101,6 @@
     kept_ref,
     away_ref,
     own_ref,
-    count_ref,
     time_ref,
     rows_ref,
     fourier_ref,
@@ -123,13 +123,14 @@
     sems,
 ):
     pixels = field_ref.shape[0]
-    row_total = rows_ref.shape[0]
-    col_total = cols_ref.shape[0]
+    row_total = rows_hbm.shape[0]
+    col_total = cols_hbm.shape[0]
     own_rows = row_total // seg_total
     width = 2 * pixels // seg_total
     pairs = seg_total // 2
     block_rows = pixels // coil_total
     groups = coil_total // 2
+    cuts = [0] + [pixels * cut // 384 for cut in CUTS]
     segment = lax.axis_index("seg")
     member = lax.axis_index("coil")
 
@@ -137,15 +138,14 @@
         pltpu.make_async_copy(source, target, sems.at[i])
         for i, (source, target) in enumerate(
             (
+                (field_hbm, field_ref),
+                (cols_hbm, cols_ref),
+                (fourier_hbm, fourier_ref),
                 (rows_hbm, rows_ref),
-                (fourier_hbm, fourier_ref),
-                (cols_hbm, cols_ref),
                 (time_hbm, time_ref),
-                (field_hbm, field_ref),
+                (image_hbm, image_ref),
                 (maps_hbm, maps_ref),
-                (image_hbm, image_ref),
                 (measured_hbm, measured_ref),
-                (count_hbm, count_ref),
             )
         )
     ]
@@ -154,10 +154,31 @@
     for copy in copies[:5]:
         copy.wait()
 
-    fourier = fourier_ref[...]
-    row_op = dot(rows_ref[...], fourier).astype(jnp.bfloat16)
-    row_ref[...] = row_op
-    col_op = dot(cols_ref[...], fourier).astype(jnp.bfloat16)
+    def phases(first, last):
+        for low in range(first, last, PIECE):
+            rows = slice(low, low + PIECE)
+            sine, cosine = half_angle(field_ref[rows, :])
+            twice = 4.0 * (cosine * cosine) - 2.0
+            previous = (cosine, -sine)
+            for pair in range(pairs):
+                if pair == 1:
+                    previous, cosine, sine = (
+                        (cosine, sine),
+                        twice * cosine - cosine,
+                        twice * sine + sine,
+                    )
+                elif pair:
+                    previous, cosine, sine = (
+                        (cosine, sine),
+                        twice * cosine - previous[0],
+                        twice * sine - previous[1],
+                    )
+                phase_ref[2 * pair, rows, :] = cosine
+                phase_ref[2 * pair + 1, rows, :] = sine
+
+    early = EARLY * pixels // 384 // PIECE * PIECE
+    col_op = dot(cols_ref[...], fourier_ref[...]).astype(jnp.bfloat16)
+    phases(0, early // 2 // PIECE * PIECE)
     left_ref[:col_total, :pixels] = col_op[:, :pixels]
     left_ref[:col_total, pixels:] = -col_op[:, pixels:]
     left_ref[col_total:, :pixels] = col_op[:, pixels:]
@@ -168,27 +189,9 @@
     right_ref[:pixels, col_total:] = col_im
     right_ref[pixels:, :col_total] = -col_im
     right_ref[pixels:, col_total:] = col_re
-
-    for low in range(0, pixels, PIECE):
-        rows = slice(low, low + PIECE)
-        sine, cosine = half_angle(field_ref[rows, :])
-        twice = 4.0 * (cosine * cosine) - 2.0
-        previous = (cosine, -sine)
-        for pair in range(pairs):
-            if pair == 1:
-                previous, cosine, sine = (
-                    (cosine, sine),
-                    twice * cosine - cosine,
-                    twice * sine + sine,
-                )
-            elif pair:
-                previous, cosine, sine = (
-                    (cosine, sine),
-                    twice * cosine - previous[0],
-                    twice * sine - previous[1],
-                )
-            phase_ref[2 * pair, rows, :] = cosine
-            phase_ref[2 * pair + 1, rows, :] = sine
+    row_op = dot(rows_ref[...], fourier_ref[...]).astype(jnp.bfloat16)
+    row_ref[...] = row_op
+    phases(early // 2 // PIECE * PIECE, early)
 
     steps = jnp.broadcast_to(time_ref[...].astype(jnp.float32), (8, row_total))
 
@@ -199,20 +202,20 @@
     for pair in range(pairs):
         above, below = weight(pairs + pair), weight(pairs - 1 - pair)
         along += [above + below, above - below]
+    for copy in copies[5:]:
+        copy.wait()
     for part in range(2):
         adjoint = jnp.transpose(row_op[:, part * pixels : (part + 1) * pixels])
         columns = slice(part * row_total, (part + 1) * row_total)
         for i in range(seg_total):
             scaled = adjoint * along[i][:1].astype(jnp.bfloat16)
-            for half in range(pixels // HALF):
-                scaled_ref[half, i * HALF : (i + 1) * HALF, columns] = scaled[
-                    half * HALF : (half + 1) * HALF
-                ]
-
-    for copy in copies[5:7]:
-        copy.wait()
+            for first, last in zip(cuts, cuts[1:]):
+                base = first * seg_total + i * (last - first)
+                scaled_ref[base : base + last - first, columns] = scaled[first:last]
+
     right = right_ref[...]
     for chunk in range(pixels // CHUNK):
+        phases(max(early, chunk * CHUNK), max(early, (chunk + 1) * CHUNK))
         for low in range(0, CHUNK, PIECE):
             rows = slice(chunk * CHUNK + low, chunk * CHUNK + low + PIECE)
             image_re, image_im = image_ref[rows, :pixels], image_ref[rows, pixels:]
@@ -233,23 +236,25 @@
             piece = v[i * CHUNK : (i + 1) * CHUNK]
             first = slice(chunk * CHUNK, (chunk + 1) * CHUNK)
             second = slice(pixels + first.start, pixels + first.stop)
-            inner_ref[i, first, :] = piece
-            inner_ref[i, second, :col_total] = -piece[:, col_total:]
-            inner_ref[i, second, col_total:] = piece[:, :col_total]
+            lanes = i % 2 * 2 * col_total
+            middle, end = lanes + col_total, lanes + 2 * col_total
+            inner_ref[i // 2, first, lanes:end] = piece
+            inner_ref[i // 2, second, lanes:middle] = -piece[:, col_total:]
+            inner_ref[i // 2, second, middle:end] = piece[:, :col_total]
     samples = None
-    for i in range(seg_total):
-        y = dot(row_ref[...], inner_ref[i]) * jnp.transpose(along[i])[:, :1]
-        samples = y if samples is None else samples + y
-
-    copies[7].wait()
-    copies[8].wait()
+    for pair in range(pairs):
+        y = dot(row_ref[...], inner_ref[pair])
+        for i in range(2):
+            part = y[:, i * 2 * col_total : (i + 1) * 2 * col_total]
+            part = part * jnp.transpose(along[2 * pair + i])[:, :1]
+            samples = part if samples is None else samples + part
+
     row_ids = lax.broadcasted_iota(jnp.int32, (row_total, 2 * col_total), 0)
     misfit = samples - measured_ref[...].astype(jnp.float32)
-    misfit = jnp.where(row_ids < count_ref[...], misfit, 0.0)
+    misfit = jnp.where(row_ids < count_ref[0], misfit, 0.0)
     misfit_ref[...] = misfit
     own_start = pl.multiple_of(segment * own_rows, own_rows)
-    own_copy = pltpu.make_async_copy(misfit_ref.at[pl.ds(own_start, own_rows)], own_ref, sems.at[9])
-    own_copy.start()
+    own_ref[...] = misfit_ref[pl.ds(own_start, own_rows), :]
 
     column = lax.rem(segment * width, pixels)
     imaginary = segment * width >= pixels
@@ -266,27 +271,30 @@
     turned_ref[row_total:, WINDOW:] = -turn_re
     turned = turned_ref[...]
     factor = coil_total ** (-0.5)
-    for half in range(pixels // HALF):
-        back_ref[half] = dot(scaled_ref[half], turned)
-        for low in range(0, HALF, PIECE):
-            rows = slice(half * HALF + low, half * HALF + low + PIECE)
+    for first, last in zip(cuts, cuts[1:]):
+        tall = last - first
+        part = slice(first * seg_total, last * seg_total)
+        back_ref[part, :] = dot(scaled_ref[part, :], turned)
+        for low in range(0, tall, PIECE):
+            rows = slice(first + low, first + low + PIECE)
             sum_re = None
             for pair in range(pairs):
                 cosine = phase_ref[2 * pair, rows, pl.ds(start, WINDOW)]
                 sine = phase_ref[2 * pair + 1, rows, pl.ds(start, WINDOW)]
-                even = slice(2 * pair * HALF + low, 2 * pair * HALF + low + PIECE)
-                odd = slice(even.start + HALF, even.stop + HALF)
-                add_re = cosine * back_ref[half, even, :WINDOW]
-                add_re = add_re + sine * back_ref[half, odd, WINDOW:]
-                add_im = cosine * back_ref[half, even, WINDOW:]
-                add_im = add_im - sine * back_ref[half, odd, :WINDOW]
+                base = first * seg_total + 2 * pair * tall + low
+                even = slice(base, base + PIECE)
+                odd = slice(base + tall, base + tall + PIECE)
+                add_re = cosine * back_ref[even, :WINDOW]
+                add_re = add_re + sine * back_ref[odd, WINDOW:]
+                add_im = cosine * back_ref[even, WINDOW:]
+                add_im = add_im - sine * back_ref[odd, :WINDOW]
                 sum_re = add_re if sum_re is None else sum_re + add_re
                 sum_im = add_im if pair == 0 else sum_im + add_im
             map_re = maps_ref[rows, pl.ds(start, WINDOW)].astype(jnp.float32)
             map_im = maps_ref[rows, pl.ds(after, WINDOW)].astype(jnp.float32)
-            first = jnp.where(imaginary, -map_im, map_re) * factor
-            second = jnp.where(imaginary, map_re, map_im) * factor
-            term_ref[rows, :] = pltpu.roll(first * sum_re + second * sum_im, shift, 1)
+            for_re = jnp.where(imaginary, -map_im, map_re) * factor
+            for_im = jnp.where(imaginary, map_re, map_im) * factor
+            term_ref[rows, :] = pltpu.roll(for_re * sum_re + for_im * sum_im, shift, 1)
 
     lane = lax.rem(member, 2)
     group = member // 2
@@ -302,7 +310,6 @@
             for piece in pack(value):
                 ref[slot, top : top + piece.shape[0], :] = piece
                 top += piece.shape[0]
-    own_copy.wait()
 
 
 def local_terms(seg_total, coil_total, image, maps, field, rows, cols, measured, time, count):
@@ -312,6 +319,7 @@
     fourier = jnp.asarray(dft_tables(pixels), jnp.bfloat16)
     anywhere = pl.BlockSpec(memory_space=pl.ANY)
     vmem = pl.BlockSpec(memory_space=pltpu.VMEM)
+    smem = pl.BlockSpec(memory_space=pltpu.SMEM)
     operands = (time, rows, fourier, cols, field, maps, image, measured)
     blocks = (coil_total // 2, *packed_shape(pixels // coil_total, width))
     return pl.pallas_call(
@@ -319,24 +327,24 @@
         out_shape=(
             pltpu.VMEM(blocks, jnp.float32),
             pltpu.VMEM(blocks, jnp.float32),
-            jax.ShapeDtypeStruct((row_total // seg_total, 2 * col_total), jnp.float32),
+            pltpu.VMEM((row_total // seg_total, 2 * col_total), jnp.float32),
         ),
-        in_specs=[anywhere] * (1 + len(operands)),
-        out_specs=(vmem, vmem, anywhere),
-        scratch_shapes=[pltpu.VMEM(x.shape, x.dtype) for x in (count, *operands)]
+        in_specs=[smem] + [anywhere] * len(operands),
+        out_specs=(vmem, vmem, vmem),
+        scratch_shapes=[pltpu.VMEM(x.shape, x.dtype) for x in operands]
         + [
             pltpu.VMEM((pixels // CHUNK, seg_total * CHUNK, 2 * pixels), jnp.bfloat16),
             pltpu.VMEM((seg_total, pixels, pixels), jnp.float32),
             pltpu.VMEM((2 * col_total, 2 * pixels), jnp.bfloat16),
             pltpu.VMEM((2 * pixels, 2 * col_total), jnp.bfloat16),
-            pltpu.VMEM((seg_total, 2 * pixels, 2 * col_total), jnp.bfloat16),
+            pltpu.VMEM((seg_total // 2, 2 * pixels, 4 * col_total), jnp.bfloat16),
             pltpu.VMEM((row_total, 2 * col_total), jnp.float32),
             pltpu.VMEM((row_total, 2 * pixels), jnp.bfloat16),
             pltpu.VMEM((2 * row_total, 2 * WINDOW), jnp.bfloat16),
-            pltpu.VMEM((pixels // HALF, seg_total * HALF, 2 * row_total), jnp.bfloat16),
-            pltpu.VMEM((pixels // HALF, seg_total * HALF, 2 * WINDOW), jnp.float32),
+            pltpu.VMEM((seg_total * pixels, 2 * row_total), jnp.bfloat16),
+            pltpu.VMEM((seg_total * pixels, 2 * WINDOW), jnp.float32),
             pltpu.VMEM((pixels, WINDOW), jnp.float32),
-            pltpu.SemaphoreType.DMA((10,)),
+            pltpu.SemaphoreType.DMA((8,)),
         ],
         compiler_params=pltpu.CompilerParams(vmem_limit_bytes=56 * 1024 * 1024),
         name="local_terms",
@@ -392,7 +400,7 @@
         interp_cols[0],
         measured[0, 0],
         sample_time,
-        sample_count.reshape(1, 1),
+        sample_count,
     )
     total = exchange_sum(kept, away, "coil")
     gradient = unpack(total, pixels // coil_total, 2 * pixels // seg_total)

time: 20.2 us -> 19.4 us (0.960)
  Pallas kernels: 5.75 us -> 4.91 us
  local copies, waits for them, and re-layouts: 0.09 us -> 0.72 us
  waiting for transfers between devices: 5.81 us -> 5.18 us
    pallas_call x1, Pallas kernels: 5.75 us -> 4.91 us  [local_terms(): pl.pallas_call(functools.partial(local_kernel, seg_total, coil_total), ou...]
    ppermute x3, waiting for transfers between devices: 4.8 us -> 4.17 us  [exchange_sum(): got = lax.ppermute(paired[k + 1], axis, pairs)]
    unnamed x0 -> x1, local copies, waits for them, and re-layouts: none -> 0.63 us
  transfers between devices with their start and end apart: 4 -> 4, of which waited for: 4 -> 4; matrix products, arithmetic and copies ran while one was open for 0% -> 3% of each run, Pallas kernels for 0% -> 0%
where the time goes in v6:
time: 19.4 us; the launch traced here: 19.2 us
  starting transfers between devices  6.46 us (33%)
  waiting for transfers between devices  5.18 us (27%)
  Pallas kernels  4.91 us (25%)
  between operations  1.31 us (7%)
  local copies, waits for them, and re-layouts  0.72 us (4%)
  other arithmetic  0.66 us (3%)
    ppermute x3, starting transfers between devices, exchange_sum(): got = lax.ppermute(paired[k + 1], axis, pairs)  5.91 us
    pallas_call x1, Pallas kernels, local_terms(): pl.pallas_call(functools.partial(local_kernel, seg_total, coil_total), ou...  4.91 us
    ppermute x3, waiting for transfers between devices, exchange_sum(): got = lax.ppermute(paired[k + 1], axis, pairs)  4.17 us
    ppermute x1, waiting for transfers between devices, exchange_sum(): paired = kept + lax.ppermute(away, axis, [(i, i ^ 1) for i in range(total)])  1.01 us
    unnamed x1, local copies, waits for them, and re-layouts  0.63 us
    broadcast_in_dim x1, other arithmetic, shards(): return (gradient[None], own[None, None])  0.63 us
    ppermute x1, starting transfers between devices, exchange_sum(): paired = kept + lax.ppermute(away, axis, [(i, i ^ 1) for i in range(total)])  0.55 us
  transfers between devices with their start and end apart: 4, of which 4 were waited for; matrix products, arithmetic and copies ran while one was open for 3% of the time, Pallas kernels for 0%

profile of v6, /device:TPU:0, one launch (start us, length us, event | category | flops | bytes accessed | tf_op | source)
XLA Modules:
  0.0 19.2 jit_solution(10040585010138467744)
XLA Ops:
  1.3 4.9 %local_terms.1 = (f32[4,72,128]{2,1,0:T(8,128)S(1)}, f32[4,72,128]{2,1,0:T(8,128)S(1)}, f32[64,256]{1,0:T(8,128)S(1)}) custom-call(s32[1]{0:T(128)S(6)} %copy.12.count_ref, s32[1,256]{1,0:T(1,128)} %time_hbm.1, bf16[256,384]{1,0:T(8,128)(2,1)} %bitcast.25, bf16[384,768]{1,0:T(8,128)(2,1)} %constant.2.clone.fourier_hbm, bf16[128,384]{1,0:T(8,128)(2,1)} %bitcast.27, ...), custom_call_target="tpu_custom_call" | custom-call | tf_op jit(solution)/shard_map/local_terms/pallas_call | solution.py:325
  6.2 0.5 %collective-permute-start = (f32[4,72,128]{2,1,0:T(8,128)S(1)}, f32[4,72,128]{2,1,0:T(8,128)S(1)}, u32[]{:S(2)}, u32[]{:S(2)}) collective-permute-start(f32[4,72,128]{2,1,0:T(8,128)S(1)} %get-tuple-element.6), channel_id=1, source_target_pairs={{0,1},{1,0},{2,3},{3,2},{4,5},{5,4},{6,7},{7,6},{8,9},{9,8},{10,11... | collective-permute-start | bytes 442376 | tf_op jit(solution)/shard_map/ppermute | solution.py:371
  6.8 1.0 %collective-permute-done = f32[4,72,128]{2,1,0:T(8,128)S(1)} collective-permute-done((f32[4,72,128]{2,1,0:T(8,128)S(1)}, f32[4,72,128]{2,1,0:T(8,128)S(1)}, u32[]{:S(2)}, u32[]{:S(2)}) %collective-permute-start) | collective-permute-done | bytes 147488 | tf_op jit(solution)/shard_map/ppermute | solution.py:371
  7.8 4.0 %collective-permute-start.1 = (f32[72,128]{1,0:T(8,128)S(1)}, f32[72,128]{1,0:T(8,128)S(1)}, u32[]{:S(2)}, u32[]{:S(2)}) collective-permute-start(f32[72,128]{1,0:T(8,128)S(1)} %get-tuple-element.8), channel_id=1, source_target_pairs={{0,4},{1,5},{2,6},{3,7},{4,2},{5,3},{6,0},{7,1},{8,12},{9,13},{10,... | collective-permute-start | bytes 110600 | tf_op jit(solution)/shard_map/ppermute | solution.py:375
  11.8 1.6 %collective-permute-start.3 = (f32[72,128]{1,0:T(8,128)S(1)}, f32[72,128]{1,0:T(8,128)S(1)}, u32[]{:S(2)}, u32[]{:S(2)}) collective-permute-start(f32[72,128]{1,0:T(8,128)S(1)} %get-tuple-element.9), channel_id=1, source_target_pairs={{0,2},{1,3},{2,0},{3,1},{4,6},{5,7},{6,4},{7,5},{8,10},{9,11},{10,... | collective-permute-start | bytes 110600 | tf_op jit(solution)/shard_map/ppermute | solution.py:375
  13.4 0.3 %collective-permute-start.2 = (f32[72,128]{1,0:T(8,128)S(1)}, f32[72,128]{1,0:T(8,128)S(1)}, u32[]{:S(2)}, u32[]{:S(2)}) collective-permute-start(f32[72,128]{1,0:T(8,128)S(1)} %get-tuple-element.10), channel_id=1, source_target_pairs={{0,6},{1,7},{2,4},{3,5},{4,0},{5,1},{6,2},{7,3},{8,14},{9,15},{10,... | collective-permute-start | bytes 110600 | tf_op jit(solution)/shard_map/ppermute | solution.py:375
  13.7 0.6 %copy.11 = f32[1,1,64,256]{3,2,1,0:T(8,128)} copy(f32[1,1,64,256]{3,2,1,0:T(8,128)S(1)} %bitcast.22) | data formatting | bytes 131072
  14.3 0.6 %collective-permute-done.1 = f32[72,128]{1,0:T(8,128)S(1)} collective-permute-done((f32[72,128]{1,0:T(8,128)S(1)}, f32[72,128]{1,0:T(8,128)S(1)}, u32[]{:S(2)}, u32[]{:S(2)}) %collective-permute-start.1) | collective-permute-done | bytes 36896 | tf_op jit(solution)/shard_map/ppermute | solution.py:375
  15.0 0.8 %collective-permute-done.3 = f32[72,128]{1,0:T(8,128)S(1)} collective-permute-done((f32[72,128]{1,0:T(8,128)S(1)}, f32[72,128]{1,0:T(8,128)S(1)}, u32[]{:S(2)}, u32[]{:S(2)}) %collective-permute-start.3) | collective-permute-done | bytes 36896 | tf_op jit(solution)/shard_map/ppermute | solution.py:375
  15.8 2.8 %collective-permute-done.2 = f32[72,128]{1,0:T(8,128)S(1)} collective-permute-done((f32[72,128]{1,0:T(8,128)S(1)}, f32[72,128]{1,0:T(8,128)S(1)}, u32[]{:S(2)}, u32[]{:S(2)}) %collective-permute-start.2) | collective-permute-done | bytes 36896 | tf_op jit(solution)/shard_map/ppermute | solution.py:375
  18.5 0.1 fusion.3
  18.6 0.6 %maximum_bitcast_fusion = f32[1,48,192]{2,1,0:T(8,128)} fusion(f32[24,64]{1,0:T(8,128)S(1)} %get-tuple-element.12, f32[24,64]{1,0:T(8,128)S(1)} %get-tuple-element.11, f32[48,128]{1,0:T(8,128)S(1)} %slice.35), kind=kLoop, calls=%fused_computation | loop fusion | flops 18432 | bytes 73728 | tf_op jit(solution)/shard_map/broadcast_in_dim | solution.py:407
  (4 shorter events, 0.0 us)
Async XLA Ops:
  6.2 1.6 %collective-permute-start = (f32[4,72,128]{2,1,0:T(8,128)S(1)}, f32[4,72,128]{2,1,0:T(8,128)S(1)}, u32[]{:S(2)}, u32[]{:S(2)}) collective-permute-start(f32[4,72,128]{2,1,0:T(8,128)S(1)} %get-tuple-element.6), channel_id=1, source_target_pairs={{0,1},{1,0},{2,3},{3,2},{4,5},{5,4},{6,7},{7,6},{8,9},{9,8},{10,11... | collective-permute-start | bytes 442376 | tf_op jit(solution)/shard_map/ppermute | solution.py:371
  7.8 7.2 %collective-permute-start.1 = (f32[72,128]{1,0:T(8,128)S(1)}, f32[72,128]{1,0:T(8,128)S(1)}, u32[]{:S(2)}, u32[]{:S(2)}) collective-permute-start(f32[72,128]{1,0:T(8,128)S(1)} %get-tuple-element.8), channel_id=1, source_target_pairs={{0,4},{1,5},{2,6},{3,7},{4,2},{5,3},{6,0},{7,1},{8,12},{9,13},{10,... | collective-permute-start | bytes 110600 | tf_op jit(solution)/shard_map/ppermute | solution.py:375
  11.8 4.0 %collective-permute-start.3 = (f32[72,128]{1,0:T(8,128)S(1)}, f32[72,128]{1,0:T(8,128)S(1)}, u32[]{:S(2)}, u32[]{:S(2)}) collective-permute-start(f32[72,128]{1,0:T(8,128)S(1)} %get-tuple-element.9), channel_id=1, source_target_pairs={{0,2},{1,3},{2,0},{3,1},{4,6},{5,7},{6,4},{7,5},{8,10},{9,11},{10,... | collective-permute-start | bytes 110600 | tf_op jit(solution)/shard_map/ppermute | solution.py:375
  13.4 5.1 %collective-permute-start.2 = (f32[72,128]{1,0:T(8,128)S(1)}, f32[72,128]{1,0:T(8,128)S(1)}, u32[]{:S(2)}, u32[]{:S(2)}) collective-permute-start(f32[72,128]{1,0:T(8,128)S(1)} %get-tuple-element.10), channel_id=1, source_target_pairs={{0,6},{1,7},{2,4},{3,5},{4,0},{5,1},{6,2},{7,3},{8,14},{9,15},{10,... | collective-permute-start | bytes 110600 | tf_op jit(solution)/shard_map/ppermute | solution.py:375

commit v7 on v6

--- a/solution.py
+++ b/solution.py
@@ -13,7 +13,7 @@
 LANES = 128
 WINDOW = 256
 CHUNK = 192
-EARLY = 256
+EARLY = 192
 CUTS = (192, 384)
 PIECE = 16
 
@@ -37,12 +37,11 @@
     5.113416832465264e-09,
 )
 COSINE = (
-    0.999999999872559,
-    -0.12499999898030063,
-    0.002604165343651872,
-    -2.170076051907257e-05,
-    9.674607230271745e-08,
-    -2.5566742521071554e-10,
+    0.9999999702593707,
+    -0.12499983471729101,
+    0.002604019482658158,
+    -2.1655414954854096e-05,
+    9.099108440040481e-08,
 )
 
 
@@ -353,28 +352,33 @@
 
 def routes(groups):
     if groups == 4:
-        return [(2, 3, 1, 0), (3, 2, 0, 1), (1, 0, 3, 2)]
+        return [(1, 2, 3, 0), (2, 3, 0, 1), (3, 0, 1, 2)]
     return [tuple((z + step) % groups for z in range(groups)) for step in range(1, groups)]
 
 
 def slot_of(target, group, groups):
+    slot = jnp.int32(groups - 1)
     if groups != 4:
-        return lax.rem(target + groups - group, groups)
-    slot = jnp.int32(0)
+        return lax.rem(target + 2 * groups - 1 - group, groups)
     for k, route in enumerate(routes(groups)):
-        slot = jnp.where(group == route.index(target), k + 1, slot)
+        slot = jnp.where(group == route.index(target), k, slot)
     return slot
 
 
 def exchange_sum(kept, away, axis):
     total = lax.axis_size(axis)
-    paired = kept + lax.ppermute(away, axis, [(i, i ^ 1) for i in range(total)])
-    result = paired[0]
-    for k, route in enumerate(routes(total // 2)):
-        pairs = [(i, 2 * route[i // 2] + i % 2) for i in range(total)]
-        got = lax.ppermute(paired[k + 1], axis, pairs)
+    last = total // 2 - 1
+    swap = [(i, i ^ 1) for i in range(total)]
+    plan = [[(i, 2 * route[i // 2] + i % 2) for i in range(total)] for route in routes(total // 2)]
+    got = lax.ppermute(away[1:last], axis, swap)
+    both = lax.ppermute(jnp.stack([kept[0], away[0]]), axis, plan[0])
+    paired = kept[1:last] + got
+    result = kept[last] + both[0]
+    for k in range(1, last):
+        got = lax.ppermute(paired[k - 1], axis, plan[k])
         result = result + got
-    return result
+    got = lax.ppermute(away[last] + both[1], axis, swap)
+    return result + got
 
 
 def shards(

time: 19.4 us -> 20.1 us (1.036)
  waiting for transfers between devices: 5.18 us -> 6.83 us
  starting transfers between devices: 6.46 us -> 5.53 us
    ppermute x4 -> x5, waiting for transfers between devices: 5.18 us -> 6.83 us  [the longest x1 4.34 us: exchange_sum(): both = lax.ppermute(jnp.stack([kept[0], away[0]]), axis, plan[0])]
    ppermute x4 -> x5, starting transfers between devices: 6.46 us -> 5.53 us  [the longest x1 3.11 us: exchange_sum(): both = lax.ppermute(jnp.stack([kept[0], away[0]]), axis, plan[0])]
  transfers between devices with their start and end apart: 4 -> 5, of which waited for: 4 -> 3; matrix products, arithmetic and copies ran while one was open for 3% -> 3% of each run, Pallas kernels for 0% -> 0%
where the time goes in v7:
time: 20.1 us; the launch traced here: 20 us
  waiting for transfers between devices  6.83 us (34%)
  starting transfers between devices  5.53 us (28%)
  Pallas kernels  4.87 us (24%)
  between operations  1.35 us (7%)
  local copies, waits for them, and re-layouts  0.73 us (4%)
  other arithmetic  0.68 us (3%)
    pallas_call x1, Pallas kernels, local_terms(): pl.pallas_call(functools.partial(local_kernel, seg_total, coil_total), ou...  4.87 us
    ppermute x1, waiting for transfers between devices, exchange_sum(): both = lax.ppermute(jnp.stack([kept[0], away[0]]), axis, plan[0])  4.34 us
    ppermute x1, starting transfers between devices, exchange_sum(): both = lax.ppermute(jnp.stack([kept[0], away[0]]), axis, plan[0])  3.11 us
    ppermute x2, waiting for transfers between devices, exchange_sum(): got = lax.ppermute(paired[k - 1], axis, plan[k])  2.48 us
    ppermute x2, starting transfers between devices, exchange_sum(): got = lax.ppermute(paired[k - 1], axis, plan[k])  2.42 us
    broadcast_in_dim x1, other arithmetic, shards(): return (gradient[None], own[None, None])  0.63 us
    unnamed x1, local copies, waits for them, and re-layouts  0.63 us
  transfers between devices with their start and end apart: 5, of which 3 were waited for; matrix products, arithmetic and copies ran while one was open for 3% of the time, Pallas kernels for 0%

profile of v7, /device:TPU:0, one launch (start us, length us, event | category | flops | bytes accessed | tf_op | source)
XLA Modules:
  0.0 20.0 jit_solution(11360087444052105362)
XLA Ops:
  1.3 4.9 %local_terms.1 = (f32[4,72,128]{2,1,0:T(8,128)S(1)}, f32[4,72,128]{2,1,0:T(8,128)S(1)}, f32[64,256]{1,0:T(8,128)S(1)}) custom-call(s32[1]{0:T(128)S(6)} %copy.12.count_ref, s32[1,256]{1,0:T(1,128)} %time_hbm.1, bf16[256,384]{1,0:T(8,128)(2,1)} %bitcast.25, bf16[384,768]{1,0:T(8,128)(2,1)} %constant.2.clone.fourier_hbm, bf16[128,384]{1,0:T(8,128)(2,1)} %bitcast.27, ...), custom_call_target="tpu_custom_call" | custom-call | tf_op jit(solution)/shard_map/local_terms/pallas_call | solution.py:324
  6.2 3.1 %collective-permute-start = (f32[2,72,128]{2,1,0:T(8,128)S(1)}, f32[2,72,128]{2,1,0:T(8,128)S(1)}, u32[]{:S(2)}, u32[]{:S(2)}) collective-permute-start(f32[2,72,128]{2,1,0:T(8,128)S(1)} %pad_maximum_fusion), channel_id=1, source_target_pairs={{0,2},{1,3},{2,4},{3,5},{4,6},{5,7},{6,0},{7,1},{8,10},{9,11},{10,... | collective-permute-start | bytes 221192 | tf_op jit(solution)/shard_map/ppermute | solution.py:374
  9.3 0.0 collective-permute-start.1
  9.3 4.3 %collective-permute-done = f32[2,72,128]{2,1,0:T(8,128)S(1)} collective-permute-done((f32[2,72,128]{2,1,0:T(8,128)S(1)}, f32[2,72,128]{2,1,0:T(8,128)S(1)}, u32[]{:S(2)}, u32[]{:S(2)}) %collective-permute-start) | collective-permute-done | bytes 73760 | tf_op jit(solution)/shard_map/ppermute | solution.py:374
  13.7 0.0 collective-permute-start.4
  13.7 0.0 collective-permute-done.1
  13.7 1.1 %collective-permute-start.2 = (f32[72,128]{1,0:T(8,128)S(1)}, f32[72,128]{1,0:T(8,128)S(1)}, u32[]{:S(2)}, u32[]{:S(2)}) collective-permute-start(f32[72,128]{1,0:T(8,128)S(1)} %get-tuple-element.8), channel_id=1, source_target_pairs={{0,4},{1,5},{2,6},{3,7},{4,0},{5,1},{6,2},{7,3},{8,12},{9,13},{10,... | collective-permute-start | bytes 110600 | tf_op jit(solution)/shard_map/ppermute | solution.py:378
  14.8 1.4 %collective-permute-start.3 = (f32[72,128]{1,0:T(8,128)S(1)}, f32[72,128]{1,0:T(8,128)S(1)}, u32[]{:S(2)}, u32[]{:S(2)}) collective-permute-start(f32[72,128]{1,0:T(8,128)S(1)} %get-tuple-element.9), channel_id=1, source_target_pairs={{0,6},{1,7},{2,0},{3,1},{4,2},{5,3},{6,4},{7,5},{8,14},{9,15},{10,... | collective-permute-start | bytes 110600 | tf_op jit(solution)/shard_map/ppermute | solution.py:378
  16.1 0.6 %copy.11 = f32[1,1,64,256]{3,2,1,0:T(8,128)} copy(f32[1,1,64,256]{3,2,1,0:T(8,128)S(1)} %bitcast.22) | data formatting | bytes 131072
  16.8 0.0 collective-permute-done.4
  16.8 2.3 %collective-permute-done.2 = f32[72,128]{1,0:T(8,128)S(1)} collective-permute-done((f32[72,128]{1,0:T(8,128)S(1)}, f32[72,128]{1,0:T(8,128)S(1)}, u32[]{:S(2)}, u32[]{:S(2)}) %collective-permute-start.2) | collective-permute-done | bytes 36896 | tf_op jit(solution)/shard_map/ppermute | solution.py:378
  19.0 0.2 %collective-permute-done.3 = f32[72,128]{1,0:T(8,128)S(1)} collective-permute-done((f32[72,128]{1,0:T(8,128)S(1)}, f32[72,128]{1,0:T(8,128)S(1)}, u32[]{:S(2)}, u32[]{:S(2)}) %collective-permute-start.3) | collective-permute-done | bytes 36896 | tf_op jit(solution)/shard_map/ppermute | solution.py:378
  19.3 0.1 fusion.5
  19.4 0.6 %maximum_bitcast_fusion = f32[1,48,192]{2,1,0:T(8,128)} fusion(f32[24,64]{1,0:T(8,128)S(1)} %get-tuple-element.11, f32[24,64]{1,0:T(8,128)S(1)} %get-tuple-element.10, f32[48,128]{1,0:T(8,128)S(1)} %slice.59), kind=kLoop, calls=%fused_computation.2 | loop fusion | flops 18432 | bytes 73728 | tf_op jit(solution)/shard_map/broadcast_in_dim | solution.py:411
  (9 shorter events, 0.1 us)
Async XLA Ops:
  6.2 7.5 %collective-permute-start = (f32[2,72,128]{2,1,0:T(8,128)S(1)}, f32[2,72,128]{2,1,0:T(8,128)S(1)}, u32[]{:S(2)}, u32[]{:S(2)}) collective-permute-start(f32[2,72,128]{2,1,0:T(8,128)S(1)} %pad_maximum_fusion), channel_id=1, source_target_pairs={{0,2},{1,3},{2,4},{3,5},{4,6},{5,7},{6,0},{7,1},{8,10},{9,11},{10,... | collective-permute-start | bytes 221192 | tf_op jit(solution)/shard_map/ppermute | solution.py:374
  9.3 4.4 %collective-permute-start.1 = (f32[2,72,128]{2,1,0:T(8,128)S(1)}, f32[2,72,128]{2,1,0:T(8,128)S(1)}, u32[]{:S(2)}, u32[]{:S(2)}) collective-permute-start(f32[2,72,128]{2,1,0:T(8,128)S(1)} %slice.47), channel_id=1, source_target_pairs={{0,1},{1,0},{2,3},{3,2},{4,5},{5,4},{6,7},{7,6},{8,9},{9,8},{10,11... | collective-permute-start | bytes 221192 | tf_op jit(solution)/shard_map/ppermute | solution.py:373
  13.7 3.1 %collective-permute-start.4 = (f32[72,128]{1,0:T(8,128)S(1)}, f32[72,128]{1,0:T(8,128)S(1)}, u32[]{:S(2)}, u32[]{:S(2)}) collective-permute-start(f32[72,128]{1,0:T(8,128)S(1)} %fusion), channel_id=1, source_target_pairs={{0,1},{1,0},{2,3},{3,2},{4,5},{5,4},{6,7},{7,6},{8,9},{9,8},{10,11... | collective-permute-start | bytes 110600 | tf_op jit(solution)/shard_map/ppermute | solution.py:380
  13.7 5.3 %collective-permute-start.2 = (f32[72,128]{1,0:T(8,128)S(1)}, f32[72,128]{1,0:T(8,128)S(1)}, u32[]{:S(2)}, u32[]{:S(2)}) collective-permute-start(f32[72,128]{1,0:T(8,128)S(1)} %get-tuple-element.8), channel_id=1, source_target_pairs={{0,4},{1,5},{2,6},{3,7},{4,0},{5,1},{6,2},{7,3},{8,12},{9,13},{10,... | collective-permute-start | bytes 110600 | tf_op jit(solution)/shard_map/ppermute | solution.py:378
  14.8 4.5 %collective-permute-start.3 = (f32[72,128]{1,0:T(8,128)S(1)}, f32[72,128]{1,0:T(8,128)S(1)}, u32[]{:S(2)}, u32[]{:S(2)}) collective-permute-start(f32[72,128]{1,0:T(8,128)S(1)} %get-tuple-element.9), channel_id=1, source_target_pairs={{0,6},{1,7},{2,0},{3,1},{4,2},{5,3},{6,4},{7,5},{8,14},{9,15},{10,... | collective-permute-start | bytes 110600 | tf_op jit(solution)/shard_map/ppermute | solution.py:378

commit v8 on v7

--- a/solution.py
+++ b/solution.py
@@ -13,7 +13,8 @@
 LANES = 128
 WINDOW = 256
 CHUNK = 192
-EARLY = 192
+EARLY = 384
+ZERO = 192
 CUTS = (192, 384)
 PIECE = 16
 
@@ -150,8 +151,7 @@
     ]
     for copy in copies:
         copy.start()
-    for copy in copies[:5]:
-        copy.wait()
+    copies[0].wait()
 
     def phases(first, last):
         for low in range(first, last, PIECE):
@@ -175,9 +175,13 @@
                 phase_ref[2 * pair, rows, :] = cosine
                 phase_ref[2 * pair + 1, rows, :] = sine
 
+    first_rows = ZERO * pixels // 384 // PIECE * PIECE
+    phases(0, first_rows)
+    for copy in copies[1:5]:
+        copy.wait()
     early = EARLY * pixels // 384 // PIECE * PIECE
     col_op = dot(cols_ref[...], fourier_ref[...]).astype(jnp.bfloat16)
-    phases(0, early // 2 // PIECE * PIECE)
+    phases(first_rows, early)
     left_ref[:col_total, :pixels] = col_op[:, :pixels]
     left_ref[:col_total, pixels:] = -col_op[:, pixels:]
     left_ref[col_total:, :pixels] = col_op[:, pixels:]
@@ -190,7 +194,6 @@
     right_ref[pixels:, col_total:] = col_re
     row_op = dot(rows_ref[...], fourier_ref[...]).astype(jnp.bfloat16)
     row_ref[...] = row_op
-    phases(early // 2 // PIECE * PIECE, early)
 
     steps = jnp.broadcast_to(time_ref[...].astype(jnp.float32), (8, row_total))
 

time: 20.1 us -> 20 us (level)
  no operation moved by 1% of the time
where the time goes in v8:
time: 20 us; the launch traced here: 19.8 us
  waiting for transfers between devices  6.83 us (34%)
  starting transfers between devices  5.53 us (28%)
  Pallas kernels  4.73 us (24%)
  between operations  1.35 us (7%)
  local copies, waits for them, and re-layouts  0.73 us (4%)
  other arithmetic  0.68 us (3%)
    pallas_call x1, Pallas kernels, local_terms(): pl.pallas_call(functools.partial(local_kernel, seg_total, coil_total), ou...  4.73 us
    ppermute x1, waiting for transfers between devices, exchange_sum(): both = lax.ppermute(jnp.stack([kept[0], away[0]]), axis, plan[0])  4.35 us
    ppermute x1, starting transfers between devices, exchange_sum(): both = lax.ppermute(jnp.stack([kept[0], away[0]]), axis, plan[0])  3.1 us
    ppermute x2, waiting for transfers between devices, exchange_sum(): got = lax.ppermute(paired[k - 1], axis, plan[k])  2.48 us
    ppermute x2, starting transfers between devices, exchange_sum(): got = lax.ppermute(paired[k - 1], axis, plan[k])  2.42 us
    broadcast_in_dim x1, other arithmetic, shards(): return (gradient[None], own[None, None])  0.63 us
    unnamed x1, local copies, waits for them, and re-layouts  0.63 us
  transfers between devices with their start and end apart: 5, of which 3 were waited for; matrix products, arithmetic and copies ran while one was open for 3% of the time, Pallas kernels for 0%

profile of v8, /device:TPU:0, one launch (start us, length us, event | category | flops | bytes accessed | tf_op | source)
XLA Modules:
  0.0 19.8 jit_solution(11787642848057207187)
XLA Ops:
  1.3 4.7 %local_terms.1 = (f32[4,72,128]{2,1,0:T(8,128)S(1)}, f32[4,72,128]{2,1,0:T(8,128)S(1)}, f32[64,256]{1,0:T(8,128)S(1)}) custom-call(s32[1]{0:T(128)S(6)} %copy.12.count_ref, s32[1,256]{1,0:T(1,128)} %time_hbm.1, bf16[256,384]{1,0:T(8,128)(2,1)} %bitcast.25, bf16[384,768]{1,0:T(8,128)(2,1)} %constant.2.clone.fourier_hbm, bf16[128,384]{1,0:T(8,128)(2,1)} %bitcast.27, ...), custom_call_target="tpu_custom_call" | custom-call | tf_op jit(solution)/shard_map/local_terms/pallas_call | solution.py:327
  6.1 3.1 %collective-permute-start = (f32[2,72,128]{2,1,0:T(8,128)S(1)}, f32[2,72,128]{2,1,0:T(8,128)S(1)}, u32[]{:S(2)}, u32[]{:S(2)}) collective-permute-start(f32[2,72,128]{2,1,0:T(8,128)S(1)} %pad_maximum_fusion), channel_id=1, source_target_pairs={{0,2},{1,3},{2,4},{3,5},{4,6},{5,7},{6,0},{7,1},{8,10},{9,11},{10,... | collective-permute-start | bytes 221192 | tf_op jit(solution)/shard_map/ppermute | solution.py:377
  9.2 0.0 collective-permute-start.1
  9.2 4.3 %collective-permute-done = f32[2,72,128]{2,1,0:T(8,128)S(1)} collective-permute-done((f32[2,72,128]{2,1,0:T(8,128)S(1)}, f32[2,72,128]{2,1,0:T(8,128)S(1)}, u32[]{:S(2)}, u32[]{:S(2)}) %collective-permute-start) | collective-permute-done | bytes 73760 | tf_op jit(solution)/shard_map/ppermute | solution.py:377
  13.5 0.0 collective-permute-start.4
  13.5 0.0 collective-permute-done.1
  13.6 1.1 %collective-permute-start.2 = (f32[72,128]{1,0:T(8,128)S(1)}, f32[72,128]{1,0:T(8,128)S(1)}, u32[]{:S(2)}, u32[]{:S(2)}) collective-permute-start(f32[72,128]{1,0:T(8,128)S(1)} %get-tuple-element.8), channel_id=1, source_target_pairs={{0,4},{1,5},{2,6},{3,7},{4,0},{5,1},{6,2},{7,3},{8,12},{9,13},{10,... | collective-permute-start | bytes 110600 | tf_op jit(solution)/shard_map/ppermute | solution.py:381
  14.7 1.3 %collective-permute-start.3 = (f32[72,128]{1,0:T(8,128)S(1)}, f32[72,128]{1,0:T(8,128)S(1)}, u32[]{:S(2)}, u32[]{:S(2)}) collective-permute-start(f32[72,128]{1,0:T(8,128)S(1)} %get-tuple-element.9), channel_id=1, source_target_pairs={{0,6},{1,7},{2,0},{3,1},{4,2},{5,3},{6,4},{7,5},{8,14},{9,15},{10,... | collective-permute-start | bytes 110600 | tf_op jit(solution)/shard_map/ppermute | solution.py:381
  16.0 0.6 %copy.11 = f32[1,1,64,256]{3,2,1,0:T(8,128)} copy(f32[1,1,64,256]{3,2,1,0:T(8,128)S(1)} %bitcast.22) | data formatting | bytes 131072
  16.6 0.0 collective-permute-done.4
  16.6 2.3 %collective-permute-done.2 = f32[72,128]{1,0:T(8,128)S(1)} collective-permute-done((f32[72,128]{1,0:T(8,128)S(1)}, f32[72,128]{1,0:T(8,128)S(1)}, u32[]{:S(2)}, u32[]{:S(2)}) %collective-permute-start.2) | collective-permute-done | bytes 36896 | tf_op jit(solution)/shard_map/ppermute | solution.py:381
  18.9 0.2 %collective-permute-done.3 = f32[72,128]{1,0:T(8,128)S(1)} collective-permute-done((f32[72,128]{1,0:T(8,128)S(1)}, f32[72,128]{1,0:T(8,128)S(1)}, u32[]{:S(2)}, u32[]{:S(2)}) %collective-permute-start.3) | collective-permute-done | bytes 36896 | tf_op jit(solution)/shard_map/ppermute | solution.py:381
  19.1 0.1 fusion.5
  19.2 0.6 %maximum_bitcast_fusion = f32[1,48,192]{2,1,0:T(8,128)} fusion(f32[24,64]{1,0:T(8,128)S(1)} %get-tuple-element.11, f32[24,64]{1,0:T(8,128)S(1)} %get-tuple-element.10, f32[48,128]{1,0:T(8,128)S(1)} %slice.59), kind=kLoop, calls=%fused_computation.2 | loop fusion | flops 18432 | bytes 73728 | tf_op jit(solution)/shard_map/broadcast_in_dim | solution.py:414
  (9 shorter events, 0.1 us)
Async XLA Ops:
  6.1 7.5 %collective-permute-start = (f32[2,72,128]{2,1,0:T(8,128)S(1)}, f32[2,72,128]{2,1,0:T(8,128)S(1)}, u32[]{:S(2)}, u32[]{:S(2)}) collective-permute-start(f32[2,72,128]{2,1,0:T(8,128)S(1)} %pad_maximum_fusion), channel_id=1, source_target_pairs={{0,2},{1,3},{2,4},{3,5},{4,6},{5,7},{6,0},{7,1},{8,10},{9,11},{10,... | collective-permute-start | bytes 221192 | tf_op jit(solution)/shard_map/ppermute | solution.py:377
  9.2 4.4 %collective-permute-start.1 = (f32[2,72,128]{2,1,0:T(8,128)S(1)}, f32[2,72,128]{2,1,0:T(8,128)S(1)}, u32[]{:S(2)}, u32[]{:S(2)}) collective-permute-start(f32[2,72,128]{2,1,0:T(8,128)S(1)} %slice.47), channel_id=1, source_target_pairs={{0,1},{1,0},{2,3},{3,2},{4,5},{5,4},{6,7},{7,6},{8,9},{9,8},{10,11... | collective-permute-start | bytes 221192 | tf_op jit(solution)/shard_map/ppermute | solution.py:376
  13.5 3.1 %collective-permute-start.4 = (f32[72,128]{1,0:T(8,128)S(1)}, f32[72,128]{1,0:T(8,128)S(1)}, u32[]{:S(2)}, u32[]{:S(2)}) collective-permute-start(f32[72,128]{1,0:T(8,128)S(1)} %fusion), channel_id=1, source_target_pairs={{0,1},{1,0},{2,3},{3,2},{4,5},{5,4},{6,7},{7,6},{8,9},{9,8},{10,11... | collective-permute-start | bytes 110600 | tf_op jit(solution)/shard_map/ppermute | solution.py:383
  13.6 5.3 %collective-permute-start.2 = (f32[72,128]{1,0:T(8,128)S(1)}, f32[72,128]{1,0:T(8,128)S(1)}, u32[]{:S(2)}, u32[]{:S(2)}) collective-permute-start(f32[72,128]{1,0:T(8,128)S(1)} %get-tuple-element.8), channel_id=1, source_target_pairs={{0,4},{1,5},{2,6},{3,7},{4,0},{5,1},{6,2},{7,3},{8,12},{9,13},{10,... | collective-permute-start | bytes 110600 | tf_op jit(solution)/shard_map/ppermute | solution.py:381
  14.7 4.5 %collective-permute-start.3 = (f32[72,128]{1,0:T(8,128)S(1)}, f32[72,128]{1,0:T(8,128)S(1)}, u32[]{:S(2)}, u32[]{:S(2)}) collective-permute-start(f32[72,128]{1,0:T(8,128)S(1)} %get-tuple-element.9), channel_id=1, source_target_pairs={{0,6},{1,7},{2,0},{3,1},{4,2},{5,3},{6,4},{7,5},{8,14},{9,15},{10,... | collective-permute-start | bytes 110600 | tf_op jit(solution)/shard_map/ppermute | solution.py:381
